TPU v7x, 256 devices: a whole 4x4x8 slice. The times are simulated.
256 devices in a mesh: gz: 64 (over y, z, core), gy: 4 (over x).
Axes of the slice: x: 4, y: 4, z: 8, core: 2. Of those that a mesh axis runs over, the one named last changes fastest.
Arguments:
- block: float32 [8, 512, 128, 256], P(None, 'gz', 'gy'), may hold values from -6 to 6
- conduct: float32 [512, 128, 256], P('gz', 'gy'), may hold values from 0.5 to 2
Outputs:
- basis: float32 [8, 512, 128, 256], P(None, 'gz', 'gy')
All inputs are finite; a program needn't handle non-finite values.
Results may differ from a plain program's by a relative error of at most 0.00021.
Values sent between devices are 32-bit elements; how exact they have to be, the bound alone decides.
No kernel may reach another device: no remote copies, remote signals or barrier semaphores. Data moves between devices by JAX's collectives and lax.ppermute only.
A program may use at most 128 MiB of HBM per device.

v0:
```python
import math

import jax
import jax.numpy as jnp
from jax import lax
from jax.sharding import PartitionSpec as P

DEG = 4


mid_point = 12.75
half_width = 11.25


def with_halo(block, sides, width):
    for axis, dim in sides:
        count = lax.axis_size(axis)
        forward = [(i, i + 1) for i in range(count - 1)]
        backward = [(target, source) for source, target in forward]
        low = lax.ppermute(
            lax.slice_in_dim(block, block.shape[dim] - width, None, axis=dim), axis, forward
        )
        high = lax.ppermute(lax.slice_in_dim(block, 0, width, axis=dim), axis, backward)
        block = jnp.concatenate([low, block, high], axis=dim)
    return block


def copy_for_each(shard, axis):
    count = lax.axis_size(axis)
    return lax.all_to_all(
        jnp.broadcast_to(shard[None], (count, *shard.shape)), axis, 0, 0, tiled=True
    )


def taken_together(shard, axis):
    everything = copy_for_each(shard, axis)
    return jnp.sum(everything, axis=0)


def stencil(padded, kpadded):
    inner = slice(1, -1)
    centre = padded[:, 1:-1, 1:-1, 1:-1]
    kcentre = kpadded[1:-1, 1:-1, 1:-1]
    shifts = [
        (slice(2, None), inner, inner),
        (slice(None, -2), inner, inner),
        (inner, slice(2, None), inner),
        (inner, slice(None, -2), inner),
        (inner, inner, slice(2, None)),
        (inner, inner, slice(None, -2)),
    ]
    total = jnp.zeros_like(centre)
    for where in shifts:
        total = total + 0.5 * (kcentre + kpadded[where]) * (centre - padded[(slice(None),) + where])
    return total


def widen_field(array):
    return jnp.pad(array, ((0, 0), (0, 0), (0, 0), (1, 1)))


def widen_coef(array):
    return jnp.pad(array, ((0, 0), (0, 0), (1, 1)))


def double_step(current, previous, kpadded, inside):
    vectors = current.shape[0]
    stacked = current if previous is None else jnp.concatenate([current, previous], 0)
    padded = with_halo(stacked, (("gz", 1), ("gy", 2)), 2)
    current_wide = padded[:vectors]
    image = stencil(widen_field(current_wide), widen_coef(kpadded))
    current_one = current_wide[:, 1:-1, 1:-1]
    if previous is None:
        middle = (image - mid_point * current_one) / half_width
    else:
        middle = 2.0 * (image - mid_point * current_one) / half_width - padded[vectors:, 1:-1, 1:-1]
    middle = middle * inside
    again = stencil(widen_field(middle), widen_coef(kpadded[1:-1, 1:-1]))
    middle_own = middle[:, 1:-1, 1:-1]
    nextone = 2.0 * (again - mid_point * middle_own) / half_width - current
    return (nextone, middle_own)


def shards(block, conduct):
    vectors, zcount, ycount, xcount = block.shape
    width, corners = (2, True)
    kpadded = with_halo(conduct, (("gz", 0), ("gy", 1)), width)
    field = block
    zglobal = lax.axis_index("gz") * zcount + jnp.arange(zcount + 2, dtype=jnp.int32) - 1
    yglobal = lax.axis_index("gy") * ycount + jnp.arange(ycount + 2, dtype=jnp.int32) - 1
    zvalid = ((zglobal >= 0) & (zglobal < zcount * lax.axis_size("gz"))).astype(jnp.float32)
    yvalid = ((yglobal >= 0) & (yglobal < ycount * lax.axis_size("gy"))).astype(jnp.float32)
    inside = (zvalid[:, None] * yvalid[None, :])[None, :, :, None]
    for passes in range(2):
        previous = None
        current = field
        for pairs in range(DEG // 2):
            current, previous = double_step(current, previous, kpadded, inside)
        field = current
    flat = field.reshape(vectors, -1)
    local_gram = jnp.dot(flat, flat.T, precision=lax.Precision.HIGHEST)
    gram = taken_together(taken_together(local_gram, "gy"), "gz")
    lower = jnp.linalg.cholesky(gram)
    inverse = lax.linalg.triangular_solve(
        lower, jnp.eye(vectors, dtype=jnp.float32), left_side=True, lower=True
    )
    total_cells = xcount * ycount * zcount * lax.axis_size("gz") * lax.axis_size("gy")
    scaled = jnp.dot(inverse, flat, precision=lax.Precision.HIGHEST) * math.sqrt(total_cells)
    return scaled.reshape(field.shape)


def solution(mesh):
    in_specs = (P(None, "gz", "gy", None), P("gz", "gy", None))
    out_specs = P(None, "gz", "gy", None)
    return jax.shard_map(shards, mesh=mesh, in_specs=in_specs, out_specs=out_specs, check_vma=False)
```

profile of v0, /device:TPU:1, one launch (start us, length us, event | category | flops | bytes accessed | tf_op | source)
XLA Modules:
  0.0 241.8 jit_solution(6229562913408521096)
XLA Ops:
  0.9 5.1 %collective-permute-start = (f32[2,32,256]{2,1,0:T(8,128)S(1)}, f32[2,32,256]{2,1,0:T(8,128)S(1)}, u32[]{:S(2)}, u32[]{:S(2)}) collective-permute-start(f32[2,32,256]{2,1,0:T(8,128)S(1)} %get-tuple-element.44), channel_id=1, source_target_pairs={{4,0},{8,4},{12,8},{16,12},{20,16},{24,20},{28,24},{32,28},{36,32}... | collective-permute-start | bytes 196616 | tf_op jit(solution)/shard_map/ppermute | solution.py:23
  6.0 1.9 collective-permute-start.1
  9.6 2.2 collective-permute-start.4
  12.2 2.9 %collective-permute-start.5 = (f32[8,2,32,256]{3,0,2,1:T(8,128)S(1)}, f32[8,2,32,256]{3,0,2,1:T(8,128)S(1)}, u32[]{:S(2)}, u32[]{:S(2)}) collective-permute-start(f32[8,2,32,256]{3,0,2,1:T(8,128)S(1)} %copy.35), channel_id=1, source_target_pairs={{4,0},{8,4},{12,8},{16,12},{20,16},{24,20},{28,24},{32,28},{36,32}... | collective-permute-start | bytes 1572872 | tf_op jit(solution)/shard_map/ppermute | solution.py:23
  15.2 2.9 %collective-permute-start.2 = (f32[12,2,256]{2,1,0:T(2,128)S(1)}, f32[12,2,256]{2,1,0:T(2,128)S(1)}, u32[]{:S(2)}, u32[]{:S(2)}) collective-permute-start(f32[12,2,256]{2,1,0:T(2,128)S(1)} %get-tuple-element.36), channel_id=1, source_target_pairs={{0,1},{1,2},{2,3},{4,5},{5,6},{6,7},{8,9},{9,10},{10,11},{12,13},{... | collective-permute-start | bytes 73736 | tf_op jit(solution)/shard_map/ppermute | solution.py:20
  19.5 3.6 %collective-permute-done.3 = f32[12,2,256]{2,1,0:T(2,128)S(1)} collective-permute-done((f32[12,2,256]{2,1,0:T(2,128)S(1)}, f32[12,2,256]{2,1,0:T(2,128)S(1)}, u32[]{:S(2)}, u32[]{:S(2)}) %collective-permute-start.3) | collective-permute-done | bytes 24608 | tf_op jit(solution)/shard_map/ppermute | solution.py:23
  23.6 2.0 constant_dynamic-update-slice_fusion.5
  27.0 3.1 %collective-permute-start.6 = (f32[8,12,2,256]{3,0,2,1:T(8,128)S(1)}, f32[8,12,2,256]{3,0,2,1:T(8,128)S(1)}, u32[]{:S(2)}, u32[]{:S(2)}) collective-permute-start(f32[8,12,2,256]{3,0,2,1:T(8,128)S(1)} %get-tuple-element.15), channel_id=1, source_target_pairs={{0,1},{1,2},{2,3},{4,5},{5,6},{6,7},{8,9},{9,10},{10,11},{12,13},{... | collective-permute-start | bytes 589832 | tf_op jit(solution)/shard_map/ppermute | solution.py:20
  31.8 2.1 collective-permute-done.6
  33.9 3.8 %collective-permute-done.7 = f32[8,12,2,256]{3,0,2,1:T(8,128)S(1)} collective-permute-done((f32[8,12,2,256]{3,0,2,1:T(8,128)S(1)}, f32[8,12,2,256]{3,0,2,1:T(8,128)S(1)}, u32[]{:S(2)}, u32[]{:S(2)}) %collective-permute-start.7) | collective-permute-done | bytes 196640 | tf_op jit(solution)/shard_map/ppermute | solution.py:23
  38.2 4.2 %fusion.5 = f32[8,10,34,256]{3,0,2,1:T(8,128)S(1)} fusion(f32[8,12,36,256]{3,0,2,1:T(8,128)S(1)} %pad_maximum_fusion.2, f32[8,12,32,256]{3,0,2,1:T(8,128)S(1)} %constant_dynamic-update-slice_fusion.3, f32[8,12,2,256]{3,0,2,1:T(8,128)S(1)} %collective-permute-done.6, f32[8,12,2,256]{3,0,2,1:T(8,128)S(1)} %collective-permute-done.7, ...), kind=kLoop, calls=%fused_computation.26 | loop fusion | flops 15319040 | bytes 20684800 | tf_op jit(solution)/shard_map/mul | solution.py:77
  42.4 5.5 %fusion.166 = (f32[8,8,32,256]{3,0,2,1:T(8,128)S(1)}, f32[8,8,32,256]{3,0,2,1:T(8,128)S(1)}) fusion(f32[8,10,34,256]{3,0,2,1:T(8,128)S(1)} %fusion.5, f32[8,8,32,256]{3,2,1,0:T(8,128)S(1)} %copy-done.9, f32[8,32,256]{2,1,0:T(8,128)S(1)} %get-tuple-element.42, f32[8,32,256]{2,1,0:T(8,128)S(1)} %get-tuple-element.43, f32[8,32,256]{2,1,0:T(8,128)S(1)} %get-tuple-element.40, ...), kind=kLoop, calls=%fused_computation.282 | loop fusion | flops 11010048 | bytes 21135360 | tf_op jit(solution)/shard_map/slice | solution.py:42
  48.1 4.1 %collective-permute-start.8 = (f32[16,2,32,256]{3,0,2,1:T(8,128)S(1)}, f32[16,2,32,256]{3,0,2,1:T(8,128)S(1)}, u32[]{:S(2)}, u32[]{:S(2)}) collective-permute-start(f32[16,2,32,256]{3,0,2,1:T(8,128)S(1)} %get-tuple-element.11), channel_id=1, source_target_pairs={{0,4},{4,8},{8,12},{12,16},{16,20},{20,24},{24,28},{28,32},{32,36}... | collective-permute-start | bytes 3145736 | tf_op jit(solution)/shard_map/ppermute | solution.py:20
  52.2 1.9 collective-permute-start.9
  54.2 9.8 %collective-permute-done.8 = f32[16,2,32,256]{3,0,2,1:T(8,128)S(1)} collective-permute-done((f32[16,2,32,256]{3,0,2,1:T(8,128)S(1)}, f32[16,2,32,256]{3,0,2,1:T(8,128)S(1)}, u32[]{:S(2)}, u32[]{:S(2)}) %collective-permute-start.8) | collective-permute-done | bytes 1048608 | tf_op jit(solution)/shard_map/ppermute | solution.py:20
  64.0 4.7 %collective-permute-done.9 = f32[16,2,32,256]{3,0,2,1:T(8,128)S(1)} collective-permute-done((f32[16,2,32,256]{3,0,2,1:T(8,128)S(1)}, f32[16,2,32,256]{3,0,2,1:T(8,128)S(1)}, u32[]{:S(2)}, u32[]{:S(2)}) %collective-permute-start.9) | collective-permute-done | bytes 1048608 | tf_op jit(solution)/shard_map/ppermute | solution.py:23
  68.7 2.5 %collective-permute-start.10 = (f32[16,12,2,256]{3,0,2,1:T(8,128)S(1)}, f32[16,12,2,256]{3,0,2,1:T(8,128)S(1)}, u32[]{:S(2)}, u32[]{:S(2)}) collective-permute-start(f32[16,12,2,256]{3,0,2,1:T(8,128)S(1)} %get-tuple-element.7), channel_id=1, source_target_pairs={{0,1},{1,2},{2,3},{4,5},{5,6},{6,7},{8,9},{9,10},{10,11},{12,13},{... | collective-permute-start | bytes 1179656 | tf_op jit(solution)/shard_map/ppermute | solution.py:20
  72.6 3.4 %collective-permute-done.10 = f32[16,12,2,256]{3,0,2,1:T(8,128)S(1)} collective-permute-done((f32[16,12,2,256]{3,0,2,1:T(8,128)S(1)}, f32[16,12,2,256]{3,0,2,1:T(8,128)S(1)}, u32[]{:S(2)}, u32[]{:S(2)}) %collective-permute-start.10) | collective-permute-done | bytes 393248 | tf_op jit(solution)/shard_map/ppermute | solution.py:20
  75.9 3.8 %collective-permute-done.11 = f32[16,12,2,256]{3,0,2,1:T(8,128)S(1)} collective-permute-done((f32[16,12,2,256]{3,0,2,1:T(8,128)S(1)}, f32[16,12,2,256]{3,0,2,1:T(8,128)S(1)}, u32[]{:S(2)}, u32[]{:S(2)}) %collective-permute-start.11) | collective-permute-done | bytes 393248 | tf_op jit(solution)/shard_map/ppermute | solution.py:23
  80.7 2.6 %slice.545 = f32[8,12,36,256]{3,0,2,1:T(8,128)} slice(f32[16,12,36,256]{3,0,2,1:T(8,128)S(1)} %pad_maximum_fusion), slice={[0:8], [0:12], [0:36], [0:256]} | slice | bytes 7077888 | tf_op jit(solution)/shard_map/slice | solution.py:70
  83.3 1.4 copy-done.3
  84.7 11.3 %fusion.15 = f32[8,10,34,256]{3,0,2,1:T(8,128)S(1)} fusion(f32[8,12,36,256]{3,0,2,1:T(8,128)} %slice.545, f32[16,12,36,256]{3,0,2,1:T(8,128)} %copy-done.3, f32[16,12,2,256]{3,0,2,1:T(8,128)} %copy-done.34, f32[16,2,32,256]{3,0,2,1:T(8,128)} %copy-done.23, f32[16,2,32,256]{3,0,2,1:T(8,128)} %copy-done.22, f32[8,8,32,256]{3,0,2,1:T(8,128)} %copy-done.7, ...), kind=kLoop, calls=%fused_computation.36 | loop fusion | flops 20889600 | bytes 26633552 | tf_op jit(solution)/shard_map/mul | solution.py:77
  96.0 4.4 %fusion.87 = f32[8,8,32,256]{3,0,2,1:T(8,128)S(1)} fusion(f32[8,8,32,256]{3,0,2,1:T(8,128)} %copy-done.1, f32[8,10,34,256]{3,0,2,1:T(8,128)S(1)} %fusion.15, f32[8,32,256]{2,1,0:T(8,128)} %copy-done.27, f32[8,32,256]{2,1,0:T(8,128)} %copy-done.28, f32[8,32,256]{2,1,0:T(8,128)} %copy-done.25, f32[8,32,256]{2,1,0:T(8,128)} %copy-done.26, ...), kind=kLoop, calls=%fused_computation.140 | loop fusion | flops 11010048 | bytes 19038208 | tf_op jit(solution)/shard_map/sub | solution.py:80
  100.5 6.4 %collective-permute-start.12 = (f32[8,2,32,256]{3,0,2,1:T(8,128)S(1)}, f32[8,2,32,256]{3,0,2,1:T(8,128)S(1)}, u32[]{:S(2)}, u32[]{:S(2)}) collective-permute-start(f32[8,2,32,256]{3,0,2,1:T(8,128)S(1)} %get-tuple-element.21), channel_id=1, source_target_pairs={{0,4},{4,8},{8,12},{12,16},{16,20},{20,24},{24,28},{28,32},{32,36}... | collective-permute-start | bytes 1572872 | tf_op jit(solution)/shard_map/ppermute | solution.py:20
  106.9 1.9 collective-permute-start.13
  108.9 4.2 %collective-permute-done.12 = f32[8,2,32,256]{3,0,2,1:T(8,128)S(1)} collective-permute-done((f32[8,2,32,256]{3,0,2,1:T(8,128)S(1)}, f32[8,2,32,256]{3,0,2,1:T(8,128)S(1)}, u32[]{:S(2)}, u32[]{:S(2)}) %collective-permute-start.12) | collective-permute-done | bytes 524320 | tf_op jit(solution)/shard_map/ppermute | solution.py:20
  113.0 4.7 %collective-permute-done.13 = f32[8,2,32,256]{3,0,2,1:T(8,128)S(1)} collective-permute-done((f32[8,2,32,256]{3,0,2,1:T(8,128)S(1)}, f32[8,2,32,256]{3,0,2,1:T(8,128)S(1)}, u32[]{:S(2)}, u32[]{:S(2)}) %collective-permute-start.13) | collective-permute-done | bytes 524320 | tf_op jit(solution)/shard_map/ppermute | solution.py:23
  117.8 1.4 collective-permute-start.14
  119.2 1.6 collective-permute-start.15
  121.7 4.0 %collective-permute-done.15 = f32[8,12,2,256]{3,0,2,1:T(8,128)S(1)} collective-permute-done((f32[8,12,2,256]{3,0,2,1:T(8,128)S(1)}, f32[8,12,2,256]{3,0,2,1:T(8,128)S(1)}, u32[]{:S(2)}, u32[]{:S(2)}) %collective-permute-start.15) | collective-permute-done | bytes 196640 | tf_op jit(solution)/shard_map/ppermute | solution.py:23
  126.9 7.0 %fusion.23 = f32[8,10,34,256]{3,0,2,1:T(8,128)S(1)} fusion(f32[8,12,36,256]{3,0,2,1:T(8,128)S(1)} %pad_maximum_fusion.3, f32[8,12,2,256]{3,0,2,1:T(8,128)S(1)} %collective-permute-done.14, f32[8,2,32,256]{3,0,2,1:T(8,128)} %copy-done.30, f32[8,8,32,256]{3,0,2,1:T(8,128)} %copy-done.4, f32[8,2,32,256]{3,0,2,1:T(8,128)} %copy-done.29, ...), kind=kLoop, calls=%fused_computation.44 | loop fusion | flops 18104320 | bytes 20684800 | tf_op jit(solution)/shard_map/mul | solution.py:77
  133.9 4.5 %fusion.165 = (f32[8,8,32,256]{3,0,2,1:T(8,128)S(1)}, f32[8,8,32,256]{3,0,2,1:T(8,128)S(1)}) fusion(f32[8,10,34,256]{3,0,2,1:T(8,128)S(1)} %fusion.23, f32[8,8,32,256]{3,0,2,1:T(8,128)S(1)} %copy-done.5, f32[8,32,256]{2,1,0:T(8,128)} %copy-done.27, f32[8,32,256]{2,1,0:T(8,128)} %copy-done.28, f32[8,32,256]{2,1,0:T(8,128)} %copy-done.25, ...), kind=kLoop, calls=%fused_computation.281 | loop fusion | flops 11010048 | bytes 21135360 | tf_op jit(solution)/shard_map/slice | solution.py:42
  138.6 4.7 %collective-permute-start.16 = (f32[16,2,32,256]{3,0,2,1:T(8,128)S(1)}, f32[16,2,32,256]{3,0,2,1:T(8,128)S(1)}, u32[]{:S(2)}, u32[]{:S(2)}) collective-permute-start(f32[16,2,32,256]{3,0,2,1:T(8,128)S(1)} %get-tuple-element.9), channel_id=1, source_target_pairs={{0,4},{4,8},{8,12},{12,16},{16,20},{20,24},{24,28},{28,32},{32,36}... | collective-permute-start | bytes 3145736 | tf_op jit(solution)/shard_map/ppermute | solution.py:20
  143.4 1.9 collective-permute-start.17
  145.3 9.8 %collective-permute-done.16 = f32[16,2,32,256]{3,0,2,1:T(8,128)S(1)} collective-permute-done((f32[16,2,32,256]{3,0,2,1:T(8,128)S(1)}, f32[16,2,32,256]{3,0,2,1:T(8,128)S(1)}, u32[]{:S(2)}, u32[]{:S(2)}) %collective-permute-start.16) | collective-permute-done | bytes 1048608 | tf_op jit(solution)/shard_map/ppermute | solution.py:20
  155.1 4.4 %collective-permute-done.17 = f32[16,2,32,256]{3,0,2,1:T(8,128)S(1)} collective-permute-done((f32[16,2,32,256]{3,0,2,1:T(8,128)S(1)}, f32[16,2,32,256]{3,0,2,1:T(8,128)S(1)}, u32[]{:S(2)}, u32[]{:S(2)}) %collective-permute-start.17) | collective-permute-done | bytes 1048608 | tf_op jit(solution)/shard_map/ppermute | solution.py:23
  159.6 1.4 collective-permute-start.18
  162.2 3.4 %collective-permute-done.18 = f32[16,12,2,256]{3,0,2,1:T(8,128)S(1)} collective-permute-done((f32[16,12,2,256]{3,0,2,1:T(8,128)S(1)}, f32[16,12,2,256]{3,0,2,1:T(8,128)S(1)}, u32[]{:S(2)}, u32[]{:S(2)}) %collective-permute-start.18) | collective-permute-done | bytes 393248 | tf_op jit(solution)/shard_map/ppermute | solution.py:20
  165.6 3.8 %collective-permute-done.19 = f32[16,12,2,256]{3,0,2,1:T(8,128)S(1)} collective-permute-done((f32[16,12,2,256]{3,0,2,1:T(8,128)S(1)}, f32[16,12,2,256]{3,0,2,1:T(8,128)S(1)}, u32[]{:S(2)}, u32[]{:S(2)}) %collective-permute-start.19) | collective-permute-done | bytes 393248 | tf_op jit(solution)/shard_map/ppermute | solution.py:23
  170.3 2.8 %copy-done.2 = f32[16,12,36,256]{3,0,2,1:T(8,128)} copy-done((f32[16,12,36,256]{3,0,2,1:T(8,128)}, f32[16,12,36,256]{3,0,2,1:T(8,128)S(1)}, u32[]{:S(2)}) %copy-start.2) | copy-done | bytes 7077912
  173.1 2.3 slice.565
  175.5 11.3 %fusion.33 = f32[8,10,34,256]{3,0,2,1:T(8,128)S(1)} fusion(f32[8,12,36,256]{3,0,2,1:T(8,128)} %slice.565, f32[16,12,36,256]{3,0,2,1:T(8,128)} %copy-done.2, f32[16,12,2,256]{3,0,2,1:T(8,128)} %copy-done.32, f32[16,2,32,256]{3,0,2,1:T(8,128)} %copy-done.21, f32[16,2,32,256]{3,0,2,1:T(8,128)} %copy-done.20, f32[8,8,32,256]{3,0,2,1:T(8,128)} %copy-done.6, ...), kind=kLoop, calls=%fused_computation.54 | loop fusion | flops 20889600 | bytes 26633552 | tf_op jit(solution)/shard_map/mul | solution.py:77
  186.7 4.4 %fusion.105 = f32[8,8,32,256]{3,0,2,1:T(8,128)S(1)} fusion(f32[8,8,32,256]{3,0,2,1:T(8,128)} %copy-done, f32[8,10,34,256]{3,0,2,1:T(8,128)S(1)} %fusion.33, f32[8,32,256]{2,1,0:T(8,128)} %copy-done.27, f32[8,32,256]{2,1,0:T(8,128)} %copy-done.28, f32[8,32,256]{2,1,0:T(8,128)} %copy-done.25, f32[8,32,256]{2,1,0:T(8,128)} %copy-done.26, ...), kind=kLoop, calls=%fused_computation.158 | loop fusion | flops 11010048 | bytes 19038208 | tf_op jit(solution)/shard_map/sub | solution.py:80
  192.5 4.7 %convolution_bitcast_fusion = f32[8,8]{1,0:T(8,128)S(1)} fusion(f32[8,8,32,256]{3,0,2,1:T(8,128)S(1)} %fusion.105), kind=kOutput, calls=%fused_computation.205 | convolution fusion | flops 50331648 | bytes 2097408 | tf_op jit(solution)/shard_map/dot_general | solution.py:101
  197.1 6.6 %all_to_all.10 = f32[4,8,8]{2,1,0:T(8,128)S(1)} all-to-all(f32[4,8,8]{2,1,0:T(8,128)S(1)} %broadcast_in_dim.5), channel_id=1, replica_groups=mesh['gz'=64,'gy'=4] {'gy'}, dimensions={0} | all-to-all | bytes 2048 | tf_op jit(solution)/shard_map/all_to_all | solution.py:30
  203.7 29.5 %all_to_all.11 = f32[64,8,8]{2,1,0:T(8,128)S(1)} all-to-all(f32[64,8,8]{2,1,0:T(8,128)S(1)} %broadcast_in_dim.6), channel_id=1, replica_groups=mesh['gz'=64,'gy'=4] {'gz'}, dimensions={0} | all-to-all | bytes 32768 | tf_op jit(solution)/shard_map/all_to_all | solution.py:30
  236.4 3.4 %convolution_multiply_fusion = f32[8,65536]{1,0:T(8,128)S(1)} fusion(f32[8,8]{1,0:T(8,128)S(1)} %fusion.161, f32[8,65536]{1,0:T(8,128)} %bitcast.20), kind=kOutput, calls=%fused_computation | convolution fusion | flops 50855936 | bytes 4194560 | tf_op jit(solution)/shard_map/dot_general | solution.py:108
  239.8 2.0 copy.29
  (125 shorter events, 19.3 us)
Async XLA Ops:
  0.0 15.1 %copy-start.31 = (f32[8,32,256]{2,1,0:T(8,128)S(1)}, f32[8,32,256]{2,1,0:T(8,128)}, u32[]{:S(2)}) copy-start(f32[8,32,256]{2,1,0:T(8,128)} %param.3) | copy-start | bytes 786436
  0.9 14.2 %collective-permute-start = (f32[2,32,256]{2,1,0:T(8,128)S(1)}, f32[2,32,256]{2,1,0:T(8,128)S(1)}, u32[]{:S(2)}, u32[]{:S(2)}) collective-permute-start(f32[2,32,256]{2,1,0:T(8,128)S(1)} %get-tuple-element.44), channel_id=1, source_target_pairs={{4,0},{8,4},{12,8},{16,12},{20,16},{24,20},{28,24},{32,28},{36,32}... | collective-permute-start | bytes 196616 | tf_op jit(solution)/shard_map/ppermute | solution.py:23
  6.0 9.1 %collective-permute-start.1 = (f32[2,32,256]{2,1,0:T(8,128)S(1)}, f32[2,32,256]{2,1,0:T(8,128)S(1)}, u32[]{:S(2)}, u32[]{:S(2)}) collective-permute-start(f32[2,32,256]{2,1,0:T(8,128)S(1)} %get-tuple-element.45), channel_id=1, source_target_pairs={{0,4},{4,8},{8,12},{12,16},{16,20},{20,24},{24,28},{28,32},{32,36}... | collective-permute-start | bytes 196616 | tf_op jit(solution)/shard_map/ppermute | solution.py:20
  9.6 14.0 %collective-permute-start.4 = (f32[8,2,32,256]{3,0,2,1:T(8,128)S(1)}, f32[8,2,32,256]{3,0,2,1:T(8,128)}, u32[]{:S(2)}, u32[]{:S(2)}) collective-permute-start(f32[8,2,32,256]{3,0,2,1:T(8,128)S(1)} %copy.34), channel_id=1, source_target_pairs={{0,4},{4,8},{8,12},{12,16},{16,20},{20,24},{24,28},{28,32},{32,36}... | collective-permute-start | bytes 1572872 | tf_op jit(solution)/shard_map/ppermute | solution.py:20
  12.2 14.8 %collective-permute-start.5 = (f32[8,2,32,256]{3,0,2,1:T(8,128)S(1)}, f32[8,2,32,256]{3,0,2,1:T(8,128)S(1)}, u32[]{:S(2)}, u32[]{:S(2)}) collective-permute-start(f32[8,2,32,256]{3,0,2,1:T(8,128)S(1)} %copy.35), channel_id=1, source_target_pairs={{4,0},{8,4},{12,8},{16,12},{20,16},{24,20},{28,24},{32,28},{36,32}... | collective-permute-start | bytes 1572872 | tf_op jit(solution)/shard_map/ppermute | solution.py:23
  15.1 8.5 %copy-start.37 = (f32[2,32,256]{2,1,0:T(8,128)}, f32[2,32,256]{2,1,0:T(8,128)S(1)}, u32[]{:S(2)}) copy-start(f32[2,32,256]{2,1,0:T(8,128)S(1)} %collective-permute-done.1) | copy-start | bytes 196612
  15.2 4.3 %collective-permute-start.2 = (f32[12,2,256]{2,1,0:T(2,128)S(1)}, f32[12,2,256]{2,1,0:T(2,128)S(1)}, u32[]{:S(2)}, u32[]{:S(2)}) collective-permute-start(f32[12,2,256]{2,1,0:T(2,128)S(1)} %get-tuple-element.36), channel_id=1, source_target_pairs={{0,1},{1,2},{2,3},{4,5},{5,6},{6,7},{8,9},{9,10},{10,11},{12,13},{... | collective-permute-start | bytes 73736 | tf_op jit(solution)/shard_map/ppermute | solution.py:20
  18.2 5.0 %collective-permute-start.3 = (f32[12,2,256]{2,1,0:T(2,128)S(1)}, f32[12,2,256]{2,1,0:T(2,128)S(1)}, u32[]{:S(2)}, u32[]{:S(2)}) collective-permute-start(f32[12,2,256]{2,1,0:T(2,128)S(1)} %get-tuple-element.37), channel_id=1, source_target_pairs={{1,0},{2,1},{3,2},{5,4},{6,5},{7,6},{9,8},{10,9},{11,10},{13,12},{... | collective-permute-start | bytes 73736 | tf_op jit(solution)/shard_map/ppermute | solution.py:23
  23.6 14.5 %copy-start.10 = (f32[10,34,256]{2,1,0:T(8,128)}, f32[10,34,256]{2,1,0:T(8,128)S(1)}, u32[]{:S(2)}) copy-start(f32[10,34,256]{2,1,0:T(8,128)S(1)} %get-tuple-element.26) | copy-start | bytes 1044484
  23.6 14.5 %copy-start.12 = (f32[10,34,256]{2,1,0:T(8,128)}, f32[10,34,256]{2,1,0:T(8,128)S(1)}, u32[]{:S(2)}) copy-start(f32[10,34,256]{2,1,0:T(8,128)S(1)} %get-tuple-element.32) | copy-start | bytes 1044484
  23.6 14.5 %copy-start.14 = (f32[10,34,256]{2,1,0:T(8,128)}, f32[10,34,256]{2,1,0:T(8,128)S(1)}, u32[]{:S(2)}) copy-start(f32[10,34,256]{2,1,0:T(8,128)S(1)} %get-tuple-element.33) | copy-start | bytes 1044484
  23.6 14.5 %copy-start.16 = (f32[10,34,256]{2,1,0:T(8,128)}, f32[10,34,256]{2,1,0:T(8,128)S(1)}, u32[]{:S(2)}) copy-start(f32[10,34,256]{2,1,0:T(8,128)S(1)} %get-tuple-element.34) | copy-start | bytes 1044484
  23.6 14.5 %copy-start.18 = (f32[10,34,256]{2,1,0:T(8,128)}, f32[10,34,256]{2,1,0:T(8,128)S(1)}, u32[]{:S(2)}) copy-start(f32[10,34,256]{2,1,0:T(8,128)S(1)} %get-tuple-element.35) | copy-start | bytes 1044484
  27.0 6.8 %collective-permute-start.6 = (f32[8,12,2,256]{3,0,2,1:T(8,128)S(1)}, f32[8,12,2,256]{3,0,2,1:T(8,128)S(1)}, u32[]{:S(2)}, u32[]{:S(2)}) collective-permute-start(f32[8,12,2,256]{3,0,2,1:T(8,128)S(1)} %get-tuple-element.15), channel_id=1, source_target_pairs={{0,1},{1,2},{2,3},{4,5},{5,6},{6,7},{8,9},{9,10},{10,11},{12,13},{... | collective-permute-start | bytes 589832 | tf_op jit(solution)/shard_map/ppermute | solution.py:20
  30.2 7.6 %collective-permute-start.7 = (f32[8,12,2,256]{3,0,2,1:T(8,128)S(1)}, f32[8,12,2,256]{3,0,2,1:T(8,128)S(1)}, u32[]{:S(2)}, u32[]{:S(2)}) collective-permute-start(f32[8,12,2,256]{3,0,2,1:T(8,128)S(1)} %get-tuple-element.16), channel_id=1, source_target_pairs={{1,0},{2,1},{3,2},{5,4},{6,5},{7,6},{9,8},{10,9},{11,10},{13,12},{... | collective-permute-start | bytes 589832 | tf_op jit(solution)/shard_map/ppermute | solution.py:23
  31.7 10.7 %copy-start.24 = (f32[8,32,256]{2,1,0:T(8,128)}, f32[8,32,256]{2,1,0:T(8,128)S(1)}, u32[]{:S(2)}) copy-start(f32[8,32,256]{2,1,0:T(8,128)S(1)} %get-tuple-element.39) | copy-start | bytes 786436
  31.7 10.7 %copy-start.25 = (f32[8,32,256]{2,1,0:T(8,128)}, f32[8,32,256]{2,1,0:T(8,128)S(1)}, u32[]{:S(2)}) copy-start(f32[8,32,256]{2,1,0:T(8,128)S(1)} %get-tuple-element.40) | copy-start | bytes 786436
  31.7 10.7 %copy-start.26 = (f32[8,32,256]{2,1,0:T(8,128)}, f32[8,32,256]{2,1,0:T(8,128)S(1)}, u32[]{:S(2)}) copy-start(f32[8,32,256]{2,1,0:T(8,128)S(1)} %get-tuple-element.41) | copy-start | bytes 786436
  31.7 10.7 %copy-start.27 = (f32[8,32,256]{2,1,0:T(8,128)}, f32[8,32,256]{2,1,0:T(8,128)S(1)}, u32[]{:S(2)}) copy-start(f32[8,32,256]{2,1,0:T(8,128)S(1)} %get-tuple-element.42) | copy-start | bytes 786436
  31.8 10.7 %copy-start.28 = (f32[8,32,256]{2,1,0:T(8,128)}, f32[8,32,256]{2,1,0:T(8,128)S(1)}, u32[]{:S(2)}) copy-start(f32[8,32,256]{2,1,0:T(8,128)S(1)} %get-tuple-element.43) | copy-start | bytes 786436
  47.9 31.9 %copy-start.1 = (f32[8,8,32,256]{3,0,2,1:T(8,128)}, f32[8,8,32,256]{3,0,2,1:T(8,128)S(1)}, u32[]{:S(2)}) copy-start(f32[8,8,32,256]{3,0,2,1:T(8,128)S(1)} %get-tuple-element.20) | copy-start | bytes 6291460
  47.9 31.9 %copy-start.7 = (f32[8,8,32,256]{3,0,2,1:T(8,128)}, f32[8,8,32,256]{3,0,2,1:T(8,128)S(1)}, u32[]{:S(2)}) copy-start(f32[8,8,32,256]{3,0,2,1:T(8,128)S(1)} %get-tuple-element.19) | copy-start | bytes 6291460
  48.1 15.9 %collective-permute-start.8 = (f32[16,2,32,256]{3,0,2,1:T(8,128)S(1)}, f32[16,2,32,256]{3,0,2,1:T(8,128)S(1)}, u32[]{:S(2)}, u32[]{:S(2)}) collective-permute-start(f32[16,2,32,256]{3,0,2,1:T(8,128)S(1)} %get-tuple-element.11), channel_id=1, source_target_pairs={{0,4},{4,8},{8,12},{12,16},{16,20},{20,24},{24,28},{28,32},{32,36}... | collective-permute-start | bytes 3145736 | tf_op jit(solution)/shard_map/ppermute | solution.py:20
  52.2 16.4 %collective-permute-start.9 = (f32[16,2,32,256]{3,0,2,1:T(8,128)S(1)}, f32[16,2,32,256]{3,0,2,1:T(8,128)S(1)}, u32[]{:S(2)}, u32[]{:S(2)}) collective-permute-start(f32[16,2,32,256]{3,0,2,1:T(8,128)S(1)} %get-tuple-element.12), channel_id=1, source_target_pairs={{4,0},{8,4},{12,8},{16,12},{20,16},{24,20},{28,24},{32,28},{36,32}... | collective-permute-start | bytes 3145736 | tf_op jit(solution)/shard_map/ppermute | solution.py:23
  64.0 15.8 %copy-start.22 = (f32[16,2,32,256]{3,0,2,1:T(8,128)}, f32[16,2,32,256]{3,0,2,1:T(8,128)S(1)}, u32[]{:S(2)}) copy-start(f32[16,2,32,256]{3,0,2,1:T(8,128)S(1)} %collective-permute-done.8) | copy-start | bytes 3145732
  68.6 11.2 %copy-start.23 = (f32[16,2,32,256]{3,0,2,1:T(8,128)}, f32[16,2,32,256]{3,0,2,1:T(8,128)S(1)}, u32[]{:S(2)}) copy-start(f32[16,2,32,256]{3,0,2,1:T(8,128)S(1)} %collective-permute-done.9) | copy-start | bytes 3145732
  68.7 7.2 %collective-permute-start.10 = (f32[16,12,2,256]{3,0,2,1:T(8,128)S(1)}, f32[16,12,2,256]{3,0,2,1:T(8,128)S(1)}, u32[]{:S(2)}, u32[]{:S(2)}) collective-permute-start(f32[16,12,2,256]{3,0,2,1:T(8,128)S(1)} %get-tuple-element.7), channel_id=1, source_target_pairs={{0,1},{1,2},{2,3},{4,5},{5,6},{6,7},{8,9},{9,10},{10,11},{12,13},{... | collective-permute-start | bytes 1179656 | tf_op jit(solution)/shard_map/ppermute | solution.py:20
  71.3 8.5 %collective-permute-start.11 = (f32[16,12,2,256]{3,0,2,1:T(8,128)S(1)}, f32[16,12,2,256]{3,0,2,1:T(8,128)S(1)}, u32[]{:S(2)}, u32[]{:S(2)}) collective-permute-start(f32[16,12,2,256]{3,0,2,1:T(8,128)S(1)} %get-tuple-element.8), channel_id=1, source_target_pairs={{1,0},{2,1},{3,2},{5,4},{6,5},{7,6},{9,8},{10,9},{11,10},{13,12},{... | collective-permute-start | bytes 1179656 | tf_op jit(solution)/shard_map/ppermute | solution.py:23
  100.4 25.4 %copy-start.4 = (f32[8,8,32,256]{3,0,2,1:T(8,128)}, f32[8,8,32,256]{3,0,2,1:T(8,128)S(1)}, u32[]{:S(2)}) copy-start(f32[8,8,32,256]{3,0,2,1:T(8,128)S(1)} %fusion.87) | copy-start | bytes 6291460
  100.5 12.6 %collective-permute-start.12 = (f32[8,2,32,256]{3,0,2,1:T(8,128)S(1)}, f32[8,2,32,256]{3,0,2,1:T(8,128)S(1)}, u32[]{:S(2)}, u32[]{:S(2)}) collective-permute-start(f32[8,2,32,256]{3,0,2,1:T(8,128)S(1)} %get-tuple-element.21), channel_id=1, source_target_pairs={{0,4},{4,8},{8,12},{12,16},{16,20},{20,24},{24,28},{28,32},{32,36}... | collective-permute-start | bytes 1572872 | tf_op jit(solution)/shard_map/ppermute | solution.py:20
  106.9 10.8 %collective-permute-start.13 = (f32[8,2,32,256]{3,0,2,1:T(8,128)S(1)}, f32[8,2,32,256]{3,0,2,1:T(8,128)S(1)}, u32[]{:S(2)}, u32[]{:S(2)}) collective-permute-start(f32[8,2,32,256]{3,0,2,1:T(8,128)S(1)} %get-tuple-element.22), channel_id=1, source_target_pairs={{4,0},{8,4},{12,8},{16,12},{20,16},{24,20},{28,24},{32,28},{36,32}... | collective-permute-start | bytes 1572872 | tf_op jit(solution)/shard_map/ppermute | solution.py:23
  113.0 12.7 %copy-start.29 = (f32[8,2,32,256]{3,0,2,1:T(8,128)}, f32[8,2,32,256]{3,0,2,1:T(8,128)S(1)}, u32[]{:S(2)}) copy-start(f32[8,2,32,256]{3,0,2,1:T(8,128)S(1)} %collective-permute-done.12) | copy-start | bytes 1572868
  117.7 8.0 %copy-start.30 = (f32[8,2,32,256]{3,0,2,1:T(8,128)}, f32[8,2,32,256]{3,0,2,1:T(8,128)S(1)}, u32[]{:S(2)}) copy-start(f32[8,2,32,256]{3,0,2,1:T(8,128)S(1)} %collective-permute-done.13) | copy-start | bytes 1572868
  117.8 4.0 %collective-permute-start.14 = (f32[8,12,2,256]{3,0,2,1:T(8,128)S(1)}, f32[8,12,2,256]{3,0,2,1:T(8,128)S(1)}, u32[]{:S(2)}, u32[]{:S(2)}) collective-permute-start(f32[8,12,2,256]{3,0,2,1:T(8,128)S(1)} %get-tuple-element.13), channel_id=1, source_target_pairs={{0,1},{1,2},{2,3},{4,5},{5,6},{6,7},{8,9},{9,10},{10,11},{12,13},{... | collective-permute-start | bytes 589832 | tf_op jit(solution)/shard_map/ppermute | solution.py:20
  119.1 7.7 %copy-start.11 = (f32[10,34,256]{2,1,0:T(8,128)S(1)}, f32[10,34,256]{2,1,0:T(8,128)}, u32[]{:S(2)}) copy-start(f32[10,34,256]{2,1,0:T(8,128)} %copy-done.10) | copy-start | bytes 1044484
  119.2 7.7 %copy-start.13 = (f32[10,34,256]{2,1,0:T(8,128)S(1)}, f32[10,34,256]{2,1,0:T(8,128)}, u32[]{:S(2)}) copy-start(f32[10,34,256]{2,1,0:T(8,128)} %copy-done.12) | copy-start | bytes 1044484
  119.2 7.7 %copy-start.15 = (f32[10,34,256]{2,1,0:T(8,128)S(1)}, f32[10,34,256]{2,1,0:T(8,128)}, u32[]{:S(2)}) copy-start(f32[10,34,256]{2,1,0:T(8,128)} %copy-done.14) | copy-start | bytes 1044484
  119.2 7.7 %copy-start.17 = (f32[10,34,256]{2,1,0:T(8,128)S(1)}, f32[10,34,256]{2,1,0:T(8,128)}, u32[]{:S(2)}) copy-start(f32[10,34,256]{2,1,0:T(8,128)} %copy-done.16) | copy-start | bytes 1044484
  119.2 7.7 %copy-start.19 = (f32[10,34,256]{2,1,0:T(8,128)S(1)}, f32[10,34,256]{2,1,0:T(8,128)}, u32[]{:S(2)}) copy-start(f32[10,34,256]{2,1,0:T(8,128)} %copy-done.18) | copy-start | bytes 1044484
  119.2 6.5 %collective-permute-start.15 = (f32[8,12,2,256]{3,0,2,1:T(8,128)S(1)}, f32[8,12,2,256]{3,0,2,1:T(8,128)S(1)}, u32[]{:S(2)}, u32[]{:S(2)}) collective-permute-start(f32[8,12,2,256]{3,0,2,1:T(8,128)S(1)} %get-tuple-element.14), channel_id=1, source_target_pairs={{1,0},{2,1},{3,2},{5,4},{6,5},{7,6},{9,8},{10,9},{11,10},{13,12},{... | collective-permute-start | bytes 589832 | tf_op jit(solution)/shard_map/ppermute | solution.py:23
  138.4 31.0 %copy-start = (f32[8,8,32,256]{3,0,2,1:T(8,128)}, f32[8,8,32,256]{3,0,2,1:T(8,128)S(1)}, u32[]{:S(2)}) copy-start(f32[8,8,32,256]{3,0,2,1:T(8,128)S(1)} %get-tuple-element.18) | copy-start | bytes 6291460
  138.4 31.0 %copy-start.6 = (f32[8,8,32,256]{3,0,2,1:T(8,128)}, f32[8,8,32,256]{3,0,2,1:T(8,128)S(1)}, u32[]{:S(2)}) copy-start(f32[8,8,32,256]{3,0,2,1:T(8,128)S(1)} %get-tuple-element.17) | copy-start | bytes 6291460
  138.6 16.5 %collective-permute-start.16 = (f32[16,2,32,256]{3,0,2,1:T(8,128)S(1)}, f32[16,2,32,256]{3,0,2,1:T(8,128)S(1)}, u32[]{:S(2)}, u32[]{:S(2)}) collective-permute-start(f32[16,2,32,256]{3,0,2,1:T(8,128)S(1)} %get-tuple-element.9), channel_id=1, source_target_pairs={{0,4},{4,8},{8,12},{12,16},{16,20},{20,24},{24,28},{28,32},{32,36}... | collective-permute-start | bytes 3145736 | tf_op jit(solution)/shard_map/ppermute | solution.py:20
  143.4 16.1 %collective-permute-start.17 = (f32[16,2,32,256]{3,0,2,1:T(8,128)S(1)}, f32[16,2,32,256]{3,0,2,1:T(8,128)S(1)}, u32[]{:S(2)}, u32[]{:S(2)}) collective-permute-start(f32[16,2,32,256]{3,0,2,1:T(8,128)S(1)} %get-tuple-element.10), channel_id=1, source_target_pairs={{4,0},{8,4},{12,8},{16,12},{20,16},{24,20},{28,24},{32,28},{36,32}... | collective-permute-start | bytes 3145736 | tf_op jit(solution)/shard_map/ppermute | solution.py:23
  155.1 14.4 %copy-start.20 = (f32[16,2,32,256]{3,0,2,1:T(8,128)}, f32[16,2,32,256]{3,0,2,1:T(8,128)S(1)}, u32[]{:S(2)}) copy-start(f32[16,2,32,256]{3,0,2,1:T(8,128)S(1)} %collective-permute-done.16) | copy-start | bytes 3145732
  159.5 10.0 %copy-start.21 = (f32[16,2,32,256]{3,0,2,1:T(8,128)}, f32[16,2,32,256]{3,0,2,1:T(8,128)S(1)}, u32[]{:S(2)}) copy-start(f32[16,2,32,256]{3,0,2,1:T(8,128)S(1)} %collective-permute-done.17) | copy-start | bytes 3145732
  159.6 6.1 %collective-permute-start.18 = (f32[16,12,2,256]{3,0,2,1:T(8,128)S(1)}, f32[16,12,2,256]{3,0,2,1:T(8,128)S(1)}, u32[]{:S(2)}, u32[]{:S(2)}) collective-permute-start(f32[16,12,2,256]{3,0,2,1:T(8,128)S(1)} %get-tuple-element.5), channel_id=1, source_target_pairs={{0,1},{1,2},{2,3},{4,5},{5,6},{6,7},{8,9},{9,10},{10,11},{12,13},{... | collective-permute-start | bytes 1179656 | tf_op jit(solution)/shard_map/ppermute | solution.py:20
  160.9 8.5 %collective-permute-start.19 = (f32[16,12,2,256]{3,0,2,1:T(8,128)S(1)}, f32[16,12,2,256]{3,0,2,1:T(8,128)S(1)}, u32[]{:S(2)}, u32[]{:S(2)}) collective-permute-start(f32[16,12,2,256]{3,0,2,1:T(8,128)S(1)} %get-tuple-element.6), channel_id=1, source_target_pairs={{1,0},{2,1},{3,2},{5,4},{6,5},{7,6},{9,8},{10,9},{11,10},{13,12},{... | collective-permute-start | bytes 1179656 | tf_op jit(solution)/shard_map/ppermute | solution.py:23
  (11 other events, 35.2 us)
where the time goes:
time: 243 us; the launch traced here: 242 us
  waiting for transfers between devices  66.5 us (27%)
  other arithmetic  58.9 us (24%)
  starting transfers between devices  51.3 us (21%)
  blocking collectives  36 us (15%)
  local copies, waits for them, and re-layouts  19.8 us (8%)
  matrix products  8.3 us (3%)
    all_to_all x2, blocking collectives, copy_for_each(): lax.all_to_all(jnp.broadcast_to(shard[None], (count, *shard.shape)), axis...  36 us
    mul x4, other arithmetic, double_step(): middle = middle * inside  33.7 us
    ppermute x10, waiting for transfers between devices, with_halo(): lax.ppermute(lax.slice_in_dim(block, block.shape[dim] - width, None, axis...  33.6 us
    ppermute x10, waiting for transfers between devices, with_halo(): lax.ppermute(lax.slice_in_dim(block, 0, width, axis=dim), axis, backward)  32.9 us
    ppermute x10, starting transfers between devices, with_halo(): lax.ppermute(lax.slice_in_dim(block, block.shape[dim] - width, None, axis...  30.8 us
    ppermute x10, starting transfers between devices, with_halo(): lax.ppermute(lax.slice_in_dim(block, 0, width, axis=dim), axis, backward)  20.5 us
    unnamed x84, local copies, waits for them, and re-layouts  10.3 us
    slice x2, other arithmetic, stencil(): centre = padded[:, 1:-1, 1:-1, 1:-1]  10 us
  transfers between devices with their start and end apart: 20, of which 15 were waited for; matrix products, arithmetic and copies ran while one was open for 2% of the time, Pallas kernels for 0%

commit v1 on v0

v1 whole, which is shorter than its diff:
```python
import functools
import math

import jax
import jax.numpy as jnp
from jax import lax
from jax.experimental import pallas as pl
from jax.experimental.pallas import tpu as pltpu
from jax.sharding import PartitionSpec as P


mid_point = 12.75
half_width = 11.25
F32 = jnp.float32
H = 4
COEFS = 4
GROUPS = (4, 4)
PAD = 8

C_FROM, D_FROM, A_FROM, B_FROM = range(4)
C_TO, D_TO, A_TO, _ = range(4, 8)
Z_ODD = 8

CORNER = [(dz, dy, high) for dz in range(1, H) for dy in range(1, H - dz + 1) for high in (0, 1)]


def call(kernel, outs, args, alias=None, scratch=(), flops=0, limit=16 << 20, space=pltpu.VMEM):
    specs = [pl.BlockSpec(memory_space=pltpu.SMEM)]
    specs += [pl.BlockSpec(memory_space=space)] * (len(args) - 1)
    return pl.pallas_call(
        kernel,
        out_shape=[jax.ShapeDtypeStruct(s, F32) for s in outs],
        in_specs=specs,
        out_specs=[pl.BlockSpec(memory_space=pltpu.VMEM)] * len(outs),
        scratch_shapes=list(scratch),
        input_output_aliases=alias or {},
        compiler_params=pltpu.CompilerParams(vmem_limit_bytes=limit),
        cost_estimate=pl.CostEstimate(flops=flops, bytes_accessed=1 << 16, transcendentals=0),
    )(*args)


def halves(value):
    width = value.shape[-1] // 2
    return value[..., :width], value[..., width:]


def lanes():
    return lax.broadcasted_iota(jnp.int32, (8, 128), 1)


def even_first(back=False):
    row, col = (lax.broadcasted_iota(jnp.int32, (256, 256), axis) for axis in ((1, 0) if back else (0, 1)))
    return jnp.where(row == 2 * (col % 128) + col // 128, 1.0, 0.0).astype(jnp.bfloat16)


def permuted(value, matrix, terms=3):
    total = None
    for term in range(terms):
        high = value.astype(jnp.bfloat16)
        moved = jnp.dot(high, matrix, preferred_element_type=F32)
        total = moved if total is None else total + moved
        if term + 1 < terms:
            value = value - high.astype(F32)
    return total


def cut_faces(where, p_ref, faces, *, nz, ny):
    a_ref, b_ref, c_ref, d_ref = faces

    def row(y, _):
        for out_ref, start in ((a_ref, where[A_FROM]), (b_ref, where[B_FROM])):
            for z in range(H):
                out_ref[z * ny + y] = p_ref[H + start + z, H + y]
        return 0

    lax.fori_loop(0, ny, row, 0, unroll=2)
    for out_ref, start in ((c_ref, where[C_FROM]), (d_ref, where[D_FROM])):
        def layer(z, _, out_ref=out_ref, start=start):
            for j in range(H):
                out_ref[z * H + j] = p_ref[H + z, H + start + j]
            return 0

        lax.fori_loop(0, nz, layer, 0, unroll=2)


def turn_kernel(where, x_ref, k_ref, p_ref, ke_ref, *rest, nz, ny):
    faces, (k_here, sems, k_sem) = rest[:4], rest[4:]
    a_ref, b_ref, c_ref, d_ref = faces
    vectors = p_ref.shape[2]
    k_copy = pltpu.make_async_copy(k_ref, k_here, k_sem)
    copies = [
        pltpu.make_async_copy(x_ref.at[v], p_ref.at[pl.ds(H, nz), pl.ds(H, ny), v, :], sems.at[v]) for v in range(vectors)
    ]
    k_copy.start()
    for copy in copies:
        copy.start()
    k_copy.wait()
    matrix = even_first()
    nx = p_ref.shape[3]
    k_turned = permuted(k_here[...].reshape(nz * ny, nx) * (1.0 / half_width), matrix)
    for z in range(nz):
        ke_ref[H + z, pl.ds(PAD + H, ny), :] = k_turned[z * ny : (z + 1) * ny]
    for copy in copies:
        copy.wait()

    for z in range(0, nz, 4):
        block = p_ref.at[pl.ds(H + z, 4), pl.ds(H, ny)]
        block[...] = permuted(block[...].reshape(4 * ny * vectors, nx), matrix).reshape(4, ny, vectors, nx)
    cut_faces(where, p_ref, faces, nz=nz, ny=ny)
    c_low = where[C_FROM] == 0
    for z in range(nz):
        low, high = ke_ref[H + z, pl.ds(PAD + H, H), :], ke_ref[H + z, pl.ds(PAD + ny, H), :]
        at = nz * H + z * H // 8
        c_ref[at, pl.ds(z * H % 8, H), :] = jnp.where(c_low, low, high)
        d_ref[at, pl.ds(z * H % 8, H), :] = jnp.where(c_low, high, low)
    for z in range(H):
        for g in range(ny // 8):
            for out_ref, start in ((a_ref, where[A_FROM]), (b_ref, where[B_FROM])):
                out_ref[H * ny + z * (ny // 8) + g] = ke_ref[H + start + z, pl.ds(PAD + H + 8 * g, 8), :]


def own_layer(where, side, dz, nz):
    low = where[Z_ODD] == 1 - side
    return jnp.where(low, dz - 1, nz - dz)


def halo_layer(where, side, dz, nz):
    low = where[Z_ODD] == 1 - side
    return jnp.where(low, H - dz, H + nz + dz - 1)


def halo_row(dy, high, ny):
    return H + ny + dy - 1 if high else H - dy


def corner_kernel(where, p_in, *rest, nz, ny, first):
    if first:
        _, cr_ref, dr_ref, p_ref, ke_ref, a_ref, b_ref = rest
    else:
        cr_ref, dr_ref, p_ref, a_ref, b_ref = rest

    def layer(z, _):
        for j in range(H):
            p_ref[H + z, where[C_TO] + j] = cr_ref[z * H + j]
            p_ref[H + z, where[D_TO] + j] = dr_ref[z * H + j]
        return 0

    lax.fori_loop(0, nz, layer, 0, unroll=2)
    for side, out_ref in enumerate((a_ref, b_ref)):
        for n, (dz, dy, high) in enumerate(CORNER):
            out_ref[n] = p_ref[H + own_layer(where, side, dz, nz), halo_row(dy, high, ny)]
    if first:
        c_low = where[C_TO] == 0
        for z in range(nz):
            at = nz * H + z * H // 8
            kc, kd = cr_ref[at, pl.ds(z * H % 8, H), :], dr_ref[at, pl.ds(z * H % 8, H), :]
            ke_ref[H + z, pl.ds(PAD, H), :] = jnp.where(c_low, kc, kd)
            ke_ref[H + z, pl.ds(PAD + H + ny, H), :] = jnp.where(c_low, kd, kc)
        for side, out_ref in enumerate((a_ref, b_ref)):
            for n, (dz, dy, high) in enumerate(CORNER):
                row = ke_ref[H + own_layer(where, side, dz, nz), pl.ds(PAD + halo_row(dy, high, ny), 1), :]
                out_ref[len(CORNER) + n // 8, pl.ds(n % 8, 1), :] = row


def fill_side(where, side, p_ref, ke_ref, face_ref, corner_ref, *, nz, ny):
    start = where[A_TO + side]

    def row(y, _):
        for z in range(H):
            p_ref[start + z, H + y] = face_ref[z * ny + y]
        return 0

    lax.fori_loop(0, ny, row, 0, unroll=4)
    for n, (dz, dy, high) in enumerate(CORNER):
        p_ref[halo_layer(where, side, dz, nz), halo_row(dy, high, ny)] = corner_ref[n]
    if ke_ref is not None:
        for z in range(H):
            for g in range(ny // 8):
                ke_ref[start + z, pl.ds(PAD + H + 8 * g, 8), :] = face_ref[H * ny + z * (ny // 8) + g]
        for n, (dz, dy, high) in enumerate(CORNER):
            row = corner_ref[len(CORNER) + n // 8, pl.ds(n % 8, 1), :]
            ke_ref[halo_layer(where, side, dz, nz), pl.ds(PAD + halo_row(dy, high, ny), 1), :] = row


def coefficients(ke_ref, coef, z0, count):
    diag_ref, wz_ref, wy_ref, wx_ref = coef
    deep, wide = diag_ref.shape[0], diag_ref.shape[1]
    lane = lanes()

    def one(i, _):
        z = z0 + i
        below, above = jnp.maximum(z - 1, 0), jnp.minimum(z + 1, deep - 1)
        for g in range(wide // 8):
            at = PAD + 8 * g
            rows = pl.ds(8 * g, 8)
            k = ke_ref[z, pl.ds(at, 8), :]
            ku = ke_ref[above, pl.ds(at, 8), :]
            kn = ke_ref[z, pl.ds(at + 1, 8), :]
            around = (ke_ref[below, pl.ds(at, 8), :] + ku) + (ke_ref[z, pl.ds(at - 1, 8), :] + kn)
            inside = k > 0
            wz_ref[z, rows, :] = jnp.where(inside & (ku > 0), k + ku, 0.0)
            wy_ref[z, rows, :] = jnp.where(inside & (kn > 0), k + kn, 0.0)
            even, odd = halves(k)
            before = jnp.where(lane == 0, 0.0, pltpu.roll(odd, 1, 1))
            after = jnp.where(lane == 127, 0.0, pltpu.roll(even, 127, 1))
            even_around, odd_around = halves(around)
            shift = 2.0 * mid_point / half_width
            in_even, in_odd = even > 0, odd > 0
            diag_ref[z, rows, pl.ds(0, 128)] = jnp.where(in_even, 6.0 * even + (even_around + (before + odd)) - shift, 0.0)
            diag_ref[z, rows, pl.ds(128, 128)] = jnp.where(in_odd, 6.0 * odd + (odd_around + (even + after)) - shift, 0.0)
            wx_ref[z, rows, pl.ds(0, 128)] = jnp.where(in_even, even + odd, 0.0)
            wx_ref[z, rows, pl.ds(128, 128)] = jnp.where(in_odd & (lane < 127), odd + after, 0.0)
        return 0

    lax.fori_loop(0, count, one, 0)


def sweep(coef, now_ref, old_ref, store, z0, zcount, y0, ycount, first, group):
    diag_ref, wz_ref, wy_ref, wx_ref = coef
    both = (pl.ds(0, 128), pl.ds(128, 128))

    def rows(y, group):
        field = lambda z, y: [now_ref[z, y, :, part] for part in both]
        weight = lambda ref, z, y: halves(ref[z, pl.ds(y, 1), :])

        def across(value, weights):
            (even, odd), (inner, outer) = value, weights
            return inner * odd + pltpu.roll(outer * odd, 1, 1), inner * even + outer * pltpu.roll(even, 127, 1)

        def fetch(n):
            z = z0 + n
            return dict(
                ends=(field(z, y - 1), field(z, y + group)),
                wy=[weight(wy_ref, z, y - 1 + r) for r in range(group + 1)],
                diag=[weight(diag_ref, z, y + r) for r in range(group)],
                old=None if first else [[old_ref[z, y + r, :, part] for part in both] for r in range(group)],
            )

        below = [field(z0 - 1, y + r) for r in range(group)]
        here = [field(z0, y + r) for r in range(group)]
        wbelow = [weight(wz_ref, z0 - 1, y + r) for r in range(group)]
        sides = [across(here[r], weight(wx_ref, z0, y + r)) for r in range(group)]
        got = fetch(0)
        for n in range(zcount):
            z = z0 + n
            above = [field(z + 1, y + r) for r in range(group)]
            wabove = [weight(wz_ref, z, y + r) for r in range(group)]
            column = [got["ends"][0], *here, got["ends"][1]]
            made = []
            for r in range(group):
                for part in range(2):
                    pulled = wabove[r][part] * above[r][part] + wbelow[r][part] * below[r][part]
                    pulled += got["wy"][r + 1][part] * column[r + 2][part] + got["wy"][r][part] * column[r][part]
                    image = got["diag"][r][part] * here[r][part] - (pulled + sides[r][part])
                    made.append((r, part, 0.5 * image if first else image - got["old"][r][part]))
            if n + 1 < zcount:
                sides = [across(above[r], weight(wx_ref, z + 1, y + r)) for r in range(group)]
                got = fetch(n + 1)
            for r, part, value in made:
                store(z, y + r, part, value)
            below, here, wbelow = here, above, wabove

    def many(i, _):
        rows(y0 + group * i, group)
        return 0

    lax.fori_loop(0, ycount // group, many, 0)
    if ycount % group:
        rows(y0 + ycount - ycount % group, ycount % group)


def steps(where, side, coef, p_ref, q_ref, last_store, *, nz, ny):
    def into(ref):
        def store(z, y, part, value):
            ref[z, y, :, pl.ds(128 * part, 128)] = value

        return store

    odd = where[Z_ODD] == 1
    for step in range(1, H + 1):
        h = H - step
        now, old = (p_ref, q_ref) if step % 2 == 1 else (q_ref, p_ref)
        store = last_store if step == H and last_store is not None else into(old)
        if side == 0:
            z0, zcount = jnp.where(odd, H - h, H + step), nz + h - step
        else:
            z0, zcount = jnp.where(odd, H + nz - step, H - h), h + step
        sweep(coef, now, old, store, z0, zcount, H - h, ny + 2 * h, step == 1, GROUPS[side])


def near_kernel(where, p_in, *rest, nz, ny, first):
    size = dict(nz=nz, ny=ny)
    if first:
        ke_in, face_ref, corner_ref, p_ref, ke_ref, q_ref, *coef = rest
        store = None
    else:
        *coef, face_ref, corner_ref, p_ref, q_ref, left_ref, right_ref, g_ref = rest
        ke_ref = None
        store = filtered_store((left_ref, right_ref), **size)
    fill_side(where, 0, p_ref, ke_ref, face_ref, corner_ref, **size)
    if first:
        coefficients(ke_ref, coef, jnp.where(where[Z_ODD] == 1, 0, H), nz + H)
    steps(where, 0, coef, p_ref, q_ref, store, **size)
    if not first:
        pairs = products((left_ref, right_ref), where[A_FROM] * ny // 8, H * ny // 8, nz * ny, None)
        for n, total in enumerate(pairs):
            g_ref[n] = total


def far_kernel(where, p_in, q_in, *rest, nz, ny, first):
    size = dict(nz=nz, ny=ny)
    if first:
        ke_in, *rest = rest
        rest = rest[COEFS:]
        face_ref, corner_ref, p_ref, q_ref, ke_ref, *rest = rest
        coef, faces = rest[:COEFS], rest[COEFS:]
        store = None
    else:
        *coef, face_ref, corner_ref, left_in, right_in, pairs_ref, p_ref, q_ref, left_ref, right_ref, g_ref = rest
        ke_ref = None
        store = filtered_store((left_ref, right_ref), **size)
    fill_side(where, 1, p_ref, ke_ref, face_ref, corner_ref, **size)
    if first:
        coefficients(ke_ref, coef, jnp.where(where[Z_ODD] == 1, H + nz - 1, 0), H + 1)
    steps(where, 1, coef, p_ref, q_ref, store, **size)
    if first:
        cut_faces(where, p_ref, faces, **size)
    else:
        sums = products((left_ref, right_ref), where[B_FROM] * ny // 8, H * ny // 8, nz * ny, pairs_ref)
        row_of = lax.broadcasted_iota(jnp.int32, g_ref.shape, 0)
        col_of = lax.broadcasted_iota(jnp.int32, g_ref.shape, 1)
        gram = jnp.zeros(g_ref.shape, F32)
        for total, (v, w) in zip(sums, PAIRS):
            here = ((row_of == v) & (col_of == w)) | ((row_of == w) & (col_of == v))
            gram = jnp.where(here, jnp.sum(total), gram)
        g_ref[...] = gram


PAIRS = [(v, w) for v in range(8) for w in range(v + 1)]


def filtered_store(outs, *, nz, ny):
    def store(z, y, part, value):
        outs[part][pl.ds((z - H) * ny + (y - H), 8, stride=nz * ny), :] = value

    return store


def products(parts, start, count, cells, initial):
    def group(i, sums):
        out = list(sums)
        for ref in parts:
            rows = [ref[pl.ds(pl.multiple_of(v * cells + (start + i) * 8, 8), 8), :] for v in range(8)]
            for n, (v, w) in enumerate(PAIRS):
                out[n] = out[n] + rows[v] * rows[w]
        return tuple(out)

    zero = [jnp.zeros((8, 128), F32) if initial is None else initial[n] for n in range(len(PAIRS))]
    return lax.fori_loop(0, count, group, tuple(zero))


def basis_kernel(g_ref, even_ref, odd_ref, out_ref, w_ref, made_ref, *, scale):
    vectors = out_ref.shape[0]

    @pl.when(pl.program_id(0) == 0)
    def _():
        row = lax.broadcasted_iota(jnp.int32, (vectors, 128), 0)
        col = lax.broadcasted_iota(jnp.int32, (vectors, 128), 1)
        gram = jnp.sum(g_ref[...], axis=0)
        both = jnp.where(col < vectors, gram, jnp.where(col - vectors == row, 1.0, 0.0))
        scales = jnp.zeros((vectors, 128), F32)
        for k in range(vectors):
            pivot_row = jnp.broadcast_to(both[k : k + 1, :], both.shape)
            pivot = jnp.broadcast_to(pivot_row[:, k : k + 1], both.shape)
            scales = jnp.where(row == k, scale * lax.rsqrt(pivot), scales)
            if k + 1 < vectors:
                factor = jnp.broadcast_to(both[:, k : k + 1], both.shape) / pivot
                both = both - jnp.where(row > k, factor, 0.0) * pivot_row
        w_ref[...] = both * scales

    have = w_ref[...]
    spread = lambda v, w: jnp.broadcast_to(have[v : v + 1, vectors + w : vectors + w + 1], (8, 128))
    weights = [[spread(v, w) for w in range(v + 1)] for v in range(vectors)]
    count = out_ref.shape[1]
    first = pl.program_id(0) * count

    def combine(i, _):
        for part, ref in enumerate((even_ref, odd_ref)):
            field = [ref[v, pl.ds(pl.multiple_of(first + i * 8, 8), 8), :] for v in range(vectors)]
            for v in range(vectors):
                total = weights[v][0] * field[0]
                for w in range(1, v + 1):
                    total = total + weights[v][w] * field[w]
                made_ref[v, pl.ds(pl.multiple_of(i * 8, 8), 8), pl.ds(part * 128, 128)] = total
        return 0

    lax.fori_loop(0, count // 8, combine, 0)
    matrix = even_first(back=True)

    made = permuted(made_ref[...].reshape(vectors * count, 256), matrix, terms=2)
    out_ref[...] = made.reshape(out_ref.shape)


def basis(gram, left, right, cells, scale):
    vectors = gram.shape[1]
    blocks = 4
    rows = cells // blocks
    return pl.pallas_call(
        functools.partial(basis_kernel, scale=scale),
        grid=(blocks,),
        out_shape=jax.ShapeDtypeStruct((vectors, cells, 256), F32),
        in_specs=[pl.BlockSpec(memory_space=pltpu.VMEM)] * 3,
        out_specs=pl.BlockSpec((vectors, rows, 256), lambda i: (0, i, 0)),
        scratch_shapes=[pltpu.VMEM((vectors, 128), F32), pltpu.VMEM((vectors, rows, 256), F32)],
        compiler_params=pltpu.CompilerParams(vmem_limit_bytes=16 << 20),
        name="basis",
    )(gram, left.reshape(vectors, cells, 128), right.reshape(vectors, cells, 128))


def shards(block, conduct):
    vectors, nz, ny, nx = block.shape
    zcount, ycount = lax.axis_size("gz"), lax.axis_size("gy")
    zi, yi = lax.axis_index("gz"), lax.axis_index("gy")
    a_pairs = ("gz", [(i, i ^ 1) for i in range(zcount)])
    b_pairs = ("gz", [(i, ((i + 1) ^ 1) - 1) for i in range(1, zcount - 1)])
    c_pairs = ("gy", [(i, i ^ 1) for i in range(ycount)])
    d_pairs = ("gy", [(i, ((i + 1) ^ 1) - 1) for i in range(1, ycount - 1)])
    zodd, yodd = zi % 2, yi % 2
    where = jnp.stack([
        (1 - yodd) * (ny - H), yodd * (ny - H), (1 - zodd) * (nz - H), zodd * (nz - H),
        (1 - yodd) * (ny + H), yodd * (ny + H), (1 - zodd) * (nz + H), zodd * (nz + H), zodd,
    ]).astype(jnp.int32)
    wide, deep = ny + 2 * H, nz + 2 * H
    row = (vectors, nx)
    cells = nz * ny
    field, ke, weights = (deep, wide, *row), (deep, wide + 2 * PAD, nx), [(deep, wide, nx)] * COEFS
    halves_shape = [(vectors * cells, nx // 2)] * 2
    corner = len(CORNER)
    kernel = lambda f, **more: functools.partial(f, nz=nz, ny=ny, **more)
    swap = lambda payload, pairs: lax.ppermute(payload, *pairs)

    def exchange(p, ke, a, b, c, d):
        c = swap(c, c_pairs)
        d = swap(d, d_pairs)
        b = swap(b, b_pairs)
        a = swap(a, a_pairs)
        first = ke is not None
        n = corner + 2 if first else corner
        keep = [field] + ([ke.shape] if first else [])
        outs = keep + [(n, *row)] * 2
        args = (where, p) + ((ke,) if first else ()) + (c, d)
        alias = {1: 0, 2: 1} if first else {1: 0}
        *kept, ac, bc = call(kernel(corner_kernel, first=first), outs, args, alias)
        ac = swap(ac, a_pairs)
        bc = swap(bc, b_pairs)
        return kept, a, b, ac, bc

    near_flops, far_flops = 20_000_000, 12_000_000
    extra_z, extra_y = H * ny // 8, nz * H // 8
    p, k, a, b, c, d = call(
        kernel(turn_kernel),
        [field, ke, (H * ny + extra_z, *row), (H * ny + extra_z, *row), (nz * H + extra_y, *row), (nz * H + extra_y, *row)],
        (where, *(pltpu.with_memory_space_constraint(arg, pltpu.HBM) for arg in (block, conduct))), space=pltpu.HBM,
        scratch=[pltpu.VMEM(conduct.shape, F32), pltpu.SemaphoreType.DMA((vectors,)), pltpu.SemaphoreType.DMA])
    (p, k), a, b, ac, bc = exchange(p, k, a, b, c, d)
    p, k, q, *coef = call(kernel(near_kernel, first=True), [field, ke, field, *weights], (where, p, k, a, ac),
                          {1: 0, 2: 1}, flops=near_flops)
    p, q, k, *rest = call(
        kernel(far_kernel, first=True),
        [field, field, ke, *weights, (H * ny, *row), (H * ny, *row), (nz * H, *row), (nz * H, *row)],
        (where, p, q, k, *coef, b, bc), {n + 1: n for n in range(3 + COEFS)}, flops=far_flops)
    coef, (a, b, c, d) = rest[:COEFS], rest[COEFS:]
    (p,), a, b, ac, bc = exchange(p, None, a, b, c, d)
    p, q, left, right, pairs = call(
        kernel(near_kernel, first=False), [field, field, *halves_shape, (len(PAIRS), 8, 128)],
        (where, p, *coef, a, ac), {1: 0}, flops=near_flops)
    _, _, left, right, gram = call(
        kernel(far_kernel, first=False), [field, field, *halves_shape, (vectors, 128)],
        (where, p, q, *coef, b, bc, left, right, pairs), {1: 0, 2: 1, COEFS + 5: 2, COEFS + 6: 3}, flops=far_flops)
    gram = sum_everywhere(gram, zcount, ycount)
    out = basis(gram, left, right, cells, math.sqrt(nx * cells * zcount * ycount))
    return out.reshape(block.shape)


def sum_everywhere(part, zcount, ycount):
    part = part + lax.ppermute(part, "gz", [(i, i ^ 1) for i in range(zcount)])
    line = 8
    planes = zcount // (2 * line)

    def flat(y, x, z, core):
        return ((y * line + z) * 2 + core) * ycount + x

    planar = [[flat(y, x, z, core) for y in range(planes) for x in range(ycount)] for z in range(line) for core in range(2)]
    part = jnp.sum(gathered(part, ("gz", "gy"), planar), axis=0)
    lines = [[(y * line + z) * 2 + core for z in range(line)] for y in range(planes) for core in range(2)]
    return gathered(part, "gz", lines)


def gathered(part, axes, groups):
    n = len(groups[0])
    copies = jnp.broadcast_to(part[None], (n, *part.shape))
    return lax.all_to_all(copies, axes, 0, 0, axis_index_groups=groups, tiled=True)


def solution(mesh):
    in_specs = (P(None, "gz", "gy", None), P("gz", "gy", None))
    out_specs = P(None, "gz", "gy", None)
    return jax.shard_map(shards, mesh=mesh, in_specs=in_specs, out_specs=out_specs, check_vma=False)
```

time: 243 us -> 105 us (0.43)
  other arithmetic: 58.9 us -> 0.02 us
  waiting for transfers between devices: 66.5 us -> 11.7 us
  Pallas kernels: 0 us -> 37.4 us
  starting transfers between devices: 51.3 us -> 24.8 us
  local copies, waits for them, and re-layouts: 19.8 us -> 0.1 us
  matrix products: 8.3 us -> 0 us
  blocking collectives: 36 us -> 29.3 us
    ppermute x20 -> x13, waiting for transfers between devices: 66.5 us -> 11.7 us  [the longest x12 10.5 us: shards(): swap = lambda payload, pairs: lax.ppermute(payload, *pairs)]
    pallas_call x0 -> x8, Pallas kernels: none -> 37.4 us  [the longest x7 32.8 us: call(): pl.pallas_call(kernel, out_shape=[jax.ShapeDtypeStruct(s, F32) for s in o...]
    mul x7 -> x0, other arithmetic: 34.3 us -> none  [the longest x4 33.7 us: double_step(): middle = middle * inside]
    ppermute x20 -> x13, starting transfers between devices: 51.3 us -> 24.8 us  [the longest x12 24.7 us: shards(): swap = lambda payload, pairs: lax.ppermute(payload, *pairs)]
    slice x7 -> x0, other arithmetic: 10.5 us -> none  [the longest x2 10 us: stencil(): centre = padded[:, 1:-1, 1:-1, 1:-1]]
    unnamed x84 -> x0, local copies, waits for them, and re-layouts: 10.3 us -> none
    sub x2 -> x0, other arithmetic: 8.78 us -> none  [double_step(): nextone = 2.0 * (again - mid_point * middle_own) / half_width - current]
    dot_general x2 -> x0, matrix products: 8.12 us -> none  [the longest x1 4.69 us: shards(): local_gram = jnp.dot(flat, flat.T, precision=lax.Precision.HIGHEST)]
  transfers between devices with their start and end apart: 20 -> 13, of which waited for: 15 -> 3; matrix products, arithmetic and copies ran while one was open for 2% -> 0% of each run, Pallas kernels for 0% -> 17%
where the time goes in v1:
time: 105 us; the launch traced here: 103 us
  Pallas kernels  37.4 us (36%)
  blocking collectives  29.3 us (28%)
  starting transfers between devices  24.8 us (24%)
  waiting for transfers between devices  11.7 us (11%)
    pallas_call x7, Pallas kernels, call(): pl.pallas_call(kernel, out_shape=[jax.ShapeDtypeStruct(s, F32) for s in o...  32.8 us
    all_to_all x2, blocking collectives, gathered(): lax.all_to_all(copies, axes, 0, 0, axis_index_groups=groups, tiled=True)  29.3 us
    ppermute x12, starting transfers between devices, shards(): swap = lambda payload, pairs: lax.ppermute(payload, *pairs)  24.7 us
    ppermute x12, waiting for transfers between devices, shards(): swap = lambda payload, pairs: lax.ppermute(payload, *pairs)  10.5 us
    pallas_call x1, Pallas kernels, basis(): pl.pallas_call(functools.partial(basis_kernel, scale=scale), grid=(blocks...  4.53 us
  transfers between devices with their start and end apart: 13, of which 3 were waited for; matrix products, arithmetic and copies ran while one was open for 0% of the time, Pallas kernels for 17%

profile of v1, /device:TPU:1, one launch (start us, length us, event | category | flops | bytes accessed | tf_op | source)
XLA Modules:
  0.0 103.4 jit_solution(13543875092572800709)
XLA Ops:
  0.0 0.1 stack.39.where
  0.1 3.7 %shard_map.28 = (f32[16,40,8,256]{3,2,1,0:T(8,128)S(1)}, f32[16,56,256]{2,1,0:T(8,128)S(1)}, f32[144,8,256]{2,1,0:T(8,128)S(1)}, f32[144,8,256]{2,1,0:T(8,128)S(...) custom-call(s32[9]{0:T(128)S(1)} %stack.39.where, f32[8,8,32,256]{3,2,1,0:T(8,128)} %x_ref.1, f32[8,32,256]{2,1,0:T(8,128)} %k_ref.1), custom_call_target="tpu_custom_call" | custom-call | bytes 65536 | tf_op jit(solution)/shard_map/pallas_call | solution.py:30
  3.8 3.3 %collective-permute-start.2 = (f32[144,8,256]{2,1,0:T(8,128)S(1)}, f32[144,8,256]{2,1,0:T(8,128)S(1)}, u32[]{:S(2)}, u32[]{:S(2)}) collective-permute-start(f32[144,8,256]{2,1,0:T(8,128)S(1)} %get-tuple-element.48), channel_id=1, source_target_pairs={{0,4},{4,0},{8,12},{12,8},{16,20},{20,16},{24,28},{28,24},{32,36},... | collective-permute-start | bytes 3538952 | tf_op jit(solution)/shard_map/ppermute | solution.py:440
  7.1 1.9 %collective-permute-start.4 = (f32[144,8,256]{2,1,0:T(8,128)S(1)}, f32[144,8,256]{2,1,0:T(8,128)S(1)}, u32[]{:S(2)}, u32[]{:S(2)}) collective-permute-start(f32[144,8,256]{2,1,0:T(8,128)S(1)} %get-tuple-element.57), channel_id=1, source_target_pairs={{4,8},{8,4},{12,16},{16,12},{20,24},{24,20},{28,32},{32,28},{36,40... | collective-permute-start | bytes 3538952 | tf_op jit(solution)/shard_map/ppermute | solution.py:440
  9.0 1.1 %collective-permute-start = (f32[36,8,256]{2,1,0:T(8,128)S(1)}, f32[36,8,256]{2,1,0:T(8,128)S(1)}, u32[]{:S(2)}, u32[]{:S(2)}) collective-permute-start(f32[36,8,256]{2,1,0:T(8,128)S(1)} %get-tuple-element.44), channel_id=1, source_target_pairs={{0,1},{1,0},{2,3},{3,2},{4,5},{5,4},{6,7},{7,6},{8,9},{9,8},{10,11... | collective-permute-start | bytes 884744 | tf_op jit(solution)/shard_map/ppermute | solution.py:440
  10.1 0.7 collective-permute-start.1
  10.8 6.3 %collective-permute-done.rest_1_ = f32[36,8,256]{2,1,0:T(8,128)S(1)} collective-permute-done((f32[36,8,256]{2,1,0:T(8,128)S(1)}, f32[36,8,256]{2,1,0:T(8,128)S(1)}, u32[]{:S(2)}, u32[]{:S(2)}) %collective-permute-start) | collective-permute-done | bytes 294944 | tf_op jit(solution)/shard_map/ppermute | solution.py:440
  17.1 0.0 collective-permute-done.1.rest_2_
  17.1 0.6 shard_map.29
  17.7 0.1 collective-permute-start.3
  17.8 4.6 %collective-permute-start.5 = (f32[14,8,256]{2,1,0:T(8,128)S(1)}, f32[14,8,256]{2,1,0:T(8,128)S(1)}, u32[]{:S(2)}, u32[]{:S(2)}) collective-permute-start(f32[14,8,256]{2,1,0:T(8,128)S(1)} %get-tuple-element.58), channel_id=1, source_target_pairs={{4,8},{8,4},{12,16},{16,12},{20,24},{24,20},{28,32},{32,28},{36,40... | collective-permute-start | bytes 344072 | tf_op jit(solution)/shard_map/ppermute | solution.py:440
  22.5 0.0 collective-permute-done.3.rest_2_
  22.5 0.0 collective-permute-done.2.rest_1_
  22.5 8.2 %shard_map.30 = (f32[16,40,8,256]{3,2,1,0:T(8,128)S(1)}, f32[16,56,256]{2,1,0:T(8,128)S(1)}, f32[16,40,8,256]{3,2,1,0:T(8,128)S(1)}, f32[16,40,256]{2,1,0:T(8,12...) custom-call(s32[9]{0:T(128)S(1)} %stack.39.where, ...), custom_call_target="tpu_custom_call", output_to_operand_aliasing={{0}: (1, {}), {1}: (2, {})} | custom-call | flops 20000000 | bytes 65536 | tf_op jit(solution)/shard_map/pallas_call | solution.py:30
  30.7 0.0 collective-permute-done.5.rest_6_
  30.7 0.0 collective-permute-done.4.rest_5_
  30.7 5.5 %shard_map.31 = (f32[16,40,8,256]{3,2,1,0:T(8,128)S(1)}, f32[16,40,8,256]{3,2,1,0:T(8,128)S(1)}, f32[16,56,256]{2,1,0:T(8,128)S(1)}, f32[16,40,256]{2,1,0:T(8,12...) custom-call(s32[9]{0:T(128)S(1)} %stack.39.where, ...), custom_call_target="tpu_custom_call", output_to_operand_aliasing={{0}: (1, {}), {1}: (2, {}), {2}: (3, {}), {3}: (4, {}), {4}... | custom-call | flops 12000000 | bytes 65536 | tf_op jit(solution)/shard_map/pallas_call | solution.py:30
  36.3 0.1 collective-permute-start.8
  36.4 3.1 %collective-permute-start.10 = (f32[128,8,256]{2,1,0:T(8,128)S(1)}, f32[128,8,256]{2,1,0:T(8,128)S(1)}, u32[]{:S(2)}, u32[]{:S(2)}) collective-permute-start(f32[128,8,256]{2,1,0:T(8,128)S(1)} %get-tuple-element.71), channel_id=1, source_target_pairs={{4,8},{8,4},{12,16},{16,12},{20,24},{24,20},{28,32},{32,28},{36,40... | collective-permute-start | bytes 3145736 | tf_op jit(solution)/shard_map/ppermute | solution.py:440
  39.5 3.9 %collective-permute-start.6 = (f32[32,8,256]{2,1,0:T(8,128)S(1)}, f32[32,8,256]{2,1,0:T(8,128)S(1)}, u32[]{:S(2)}, u32[]{:S(2)}) collective-permute-start(f32[32,8,256]{2,1,0:T(8,128)S(1)} %get-tuple-element.60), channel_id=1, source_target_pairs={{0,1},{1,0},{2,3},{3,2},{4,5},{5,4},{6,7},{7,6},{8,9},{9,8},{10,11... | collective-permute-start | bytes 786440 | tf_op jit(solution)/shard_map/ppermute | solution.py:440
  43.4 0.7 collective-permute-start.7
  44.1 4.1 %collective-permute-done.6.rest_0_ = f32[32,8,256]{2,1,0:T(8,128)S(1)} collective-permute-done((f32[32,8,256]{2,1,0:T(8,128)S(1)}, f32[32,8,256]{2,1,0:T(8,128)S(1)}, u32[]{:S(2)}, u32[]{:S(2)}) %collective-permute-start.6) | collective-permute-done | bytes 262176 | tf_op jit(solution)/shard_map/ppermute | solution.py:440
  48.2 0.0 collective-permute-done.7.rest_1_
  48.2 0.6 shard_map.32
  48.8 0.1 collective-permute-start.9
  48.9 5.1 %collective-permute-start.11 = (f32[12,8,256]{2,1,0:T(8,128)S(1)}, f32[12,8,256]{2,1,0:T(8,128)S(1)}, u32[]{:S(2)}, u32[]{:S(2)}) collective-permute-start(f32[12,8,256]{2,1,0:T(8,128)S(1)} %get-tuple-element.72), channel_id=1, source_target_pairs={{4,8},{8,4},{12,16},{16,12},{20,24},{24,20},{28,32},{32,28},{36,40... | collective-permute-start | bytes 294920 | tf_op jit(solution)/shard_map/ppermute | solution.py:440
  54.1 0.0 collective-permute-done.9.rest_5_
  54.1 0.0 collective-permute-done.8.rest_4_
  54.1 8.2 %shard_map.33 = (f32[16,40,8,256]{3,2,1,0:T(8,128)S(1)}, f32[16,40,8,256]{3,2,1,0:T(8,128)S(1)}, f32[2048,128]{1,0:T(8,128)S(1)}, f32[2048,128]{1,0:T(8,128)S(1)}, f32[36,8,128]{2,1,0:T(8,128)S(1)}) custom-call(s32[9]{0:T(128)S(1)} %stack.39.where, f32[16,40,8,256]{3,2,1,0:T(8,128)S(1)} %get-tuple-element.62.p_in, ...), custom_call_target="tpu_custom_call", output_to_operand_aliasing={{0}: (1, {})} | custom-call | flops 20000000 | bytes 65536 | tf_op jit(solution)/shard_map/pallas_call | solution.py:30
  62.3 0.0 collective-permute-done.11.rest_5_
  62.3 0.0 collective-permute-done.10.rest_4_
  62.3 6.0 %shard_map.34 = (f32[16,40,8,256]{3,2,1,0:T(8,128)S(1)}, f32[16,40,8,256]{3,2,1,0:T(8,128)S(1)}, f32[2048,128]{1,0:T(8,128)S(1)}, f32[2048,128]{1,0:T(8,128)S(1)}, f32[8,128]{1,0:T(8,128)S(1)}) custom-call(s32[9]{0:T(128)S(1)} %stack.39.where, ...), custom_call_target="tpu_custom_call", output_to_operand_aliasing={{0}: (1, {}), {1}: (2, {}), {2}: (9, {}), {3}: (10, {})} | custom-call | flops 12000000 | bytes 65536 | tf_op jit(solution)/shard_map/pallas_call | solution.py:30
  68.3 0.1 collective-permute-start.12
  68.4 1.2 %collective-permute-done.12 = f32[8,128]{1,0:T(8,128)S(1)} collective-permute-done((f32[8,128]{1,0:T(8,128)S(1)}, f32[8,128]{1,0:T(8,128)S(1)}, u32[]{:S(2)}, u32[]{:S(2)}) %collective-permute-start.12) | collective-permute-done | bytes 4128 | tf_op jit(solution)/shard_map/ppermute | solution.py:486
  69.6 18.9 %all_to_all.10 = f32[16,8,128]{2,1,0:T(8,128)S(1)} all-to-all(f32[16,8,128]{2,1,0:T(8,128)S(1)} %broadcast_in_dim.4), channel_id=1, replica_groups={{0,1,2,3,64,65,66,67,128,129,130,131,192,193,194,195},{4,5,6,7,68,69,70..., dimensions={0} | all-to-all | bytes 131072 | tf_op jit(solution)/shard_map/all_to_all | solution.py:502
  88.5 10.4 %all_to_all.11.g_ref = f32[8,8,128]{2,1,0:T(8,128)S(1)} all-to-all(f32[8,8,128]{2,1,0:T(8,128)S(1)} %broadcast_in_dim.5), channel_id=1, replica_groups={{0,8,16,24,32,40,48,56},{4,12,20,28,36,44,52,60},{64,72,80,88,96,104,11..., dimensions={0} | all-to-all | bytes 65536 | tf_op jit(solution)/shard_map/all_to_all | solution.py:502
  98.9 4.5 %basis.1 = f32[8,256,256]{2,1,0:T(8,128)} custom-call(f32[8,8,128]{2,1,0:T(8,128)S(1)} %all_to_all.11.g_ref, f32[8,256,128]{2,1,0:T(8,128)S(1)} %bitcast.12, f32[8,256,128]{2,1,0:T(8,128)S(1)} %bitcast.13), custom_call_target="tpu_custom_call" | custom-call | tf_op jit(solution)/shard_map/basis/pallas_call | solution.py:408
  (4 shorter events, 0.0 us)
Async XLA Ops:
  3.8 18.7 %collective-permute-start.2 = (f32[144,8,256]{2,1,0:T(8,128)S(1)}, f32[144,8,256]{2,1,0:T(8,128)S(1)}, u32[]{:S(2)}, u32[]{:S(2)}) collective-permute-start(f32[144,8,256]{2,1,0:T(8,128)S(1)} %get-tuple-element.48), channel_id=1, source_target_pairs={{0,4},{4,0},{8,12},{12,8},{16,20},{20,16},{24,28},{28,24},{32,36},... | collective-permute-start | bytes 3538952 | tf_op jit(solution)/shard_map/ppermute | solution.py:440
  7.1 23.7 %collective-permute-start.4 = (f32[144,8,256]{2,1,0:T(8,128)S(1)}, f32[144,8,256]{2,1,0:T(8,128)S(1)}, u32[]{:S(2)}, u32[]{:S(2)}) collective-permute-start(f32[144,8,256]{2,1,0:T(8,128)S(1)} %get-tuple-element.57), channel_id=1, source_target_pairs={{4,8},{8,4},{12,16},{16,12},{20,24},{24,20},{28,32},{32,28},{36,40... | collective-permute-start | bytes 3538952 | tf_op jit(solution)/shard_map/ppermute | solution.py:440
  9.0 8.1 %collective-permute-start = (f32[36,8,256]{2,1,0:T(8,128)S(1)}, f32[36,8,256]{2,1,0:T(8,128)S(1)}, u32[]{:S(2)}, u32[]{:S(2)}) collective-permute-start(f32[36,8,256]{2,1,0:T(8,128)S(1)} %get-tuple-element.44), channel_id=1, source_target_pairs={{0,1},{1,0},{2,3},{3,2},{4,5},{5,4},{6,7},{7,6},{8,9},{9,8},{10,11... | collective-permute-start | bytes 884744 | tf_op jit(solution)/shard_map/ppermute | solution.py:440
  10.1 7.0 %collective-permute-start.1 = (f32[36,8,256]{2,1,0:T(8,128)S(1)}, f32[36,8,256]{2,1,0:T(8,128)S(1)}, u32[]{:S(2)}, u32[]{:S(2)}) collective-permute-start(f32[36,8,256]{2,1,0:T(8,128)S(1)} %get-tuple-element.45), channel_id=1, source_target_pairs={{1,2},{2,1},{5,6},{6,5},{9,10},{10,9},{13,14},{14,13},{17,18},{18,... | collective-permute-start | bytes 884744 | tf_op jit(solution)/shard_map/ppermute | solution.py:440
  17.7 4.8 %collective-permute-start.3 = (f32[14,8,256]{2,1,0:T(8,128)S(1)}, f32[14,8,256]{2,1,0:T(8,128)S(1)}, u32[]{:S(2)}, u32[]{:S(2)}) collective-permute-start(f32[14,8,256]{2,1,0:T(8,128)S(1)} %get-tuple-element.49), channel_id=1, source_target_pairs={{0,4},{4,0},{8,12},{12,8},{16,20},{20,16},{24,28},{28,24},{32,36},... | collective-permute-start | bytes 344072 | tf_op jit(solution)/shard_map/ppermute | solution.py:440
  17.8 12.9 %collective-permute-start.5 = (f32[14,8,256]{2,1,0:T(8,128)S(1)}, f32[14,8,256]{2,1,0:T(8,128)S(1)}, u32[]{:S(2)}, u32[]{:S(2)}) collective-permute-start(f32[14,8,256]{2,1,0:T(8,128)S(1)} %get-tuple-element.58), channel_id=1, source_target_pairs={{4,8},{8,4},{12,16},{16,12},{20,24},{24,20},{28,32},{32,28},{36,40... | collective-permute-start | bytes 344072 | tf_op jit(solution)/shard_map/ppermute | solution.py:440
  36.3 17.8 %collective-permute-start.8 = (f32[128,8,256]{2,1,0:T(8,128)S(1)}, f32[128,8,256]{2,1,0:T(8,128)S(1)}, u32[]{:S(2)}, u32[]{:S(2)}) collective-permute-start(f32[128,8,256]{2,1,0:T(8,128)S(1)} %get-tuple-element.67), channel_id=1, source_target_pairs={{0,4},{4,0},{8,12},{12,8},{16,20},{20,16},{24,28},{28,24},{32,36},... | collective-permute-start | bytes 3145736 | tf_op jit(solution)/shard_map/ppermute | solution.py:440
  36.4 25.9 %collective-permute-start.10 = (f32[128,8,256]{2,1,0:T(8,128)S(1)}, f32[128,8,256]{2,1,0:T(8,128)S(1)}, u32[]{:S(2)}, u32[]{:S(2)}) collective-permute-start(f32[128,8,256]{2,1,0:T(8,128)S(1)} %get-tuple-element.71), channel_id=1, source_target_pairs={{4,8},{8,4},{12,16},{16,12},{20,24},{24,20},{28,32},{32,28},{36,40... | collective-permute-start | bytes 3145736 | tf_op jit(solution)/shard_map/ppermute | solution.py:440
  39.5 8.7 %collective-permute-start.6 = (f32[32,8,256]{2,1,0:T(8,128)S(1)}, f32[32,8,256]{2,1,0:T(8,128)S(1)}, u32[]{:S(2)}, u32[]{:S(2)}) collective-permute-start(f32[32,8,256]{2,1,0:T(8,128)S(1)} %get-tuple-element.60), channel_id=1, source_target_pairs={{0,1},{1,0},{2,3},{3,2},{4,5},{5,4},{6,7},{7,6},{8,9},{9,8},{10,11... | collective-permute-start | bytes 786440 | tf_op jit(solution)/shard_map/ppermute | solution.py:440
  43.4 4.8 %collective-permute-start.7 = (f32[32,8,256]{2,1,0:T(8,128)S(1)}, f32[32,8,256]{2,1,0:T(8,128)S(1)}, u32[]{:S(2)}, u32[]{:S(2)}) collective-permute-start(f32[32,8,256]{2,1,0:T(8,128)S(1)} %get-tuple-element.61), channel_id=1, source_target_pairs={{1,2},{2,1},{5,6},{6,5},{9,10},{10,9},{13,14},{14,13},{17,18},{18,... | collective-permute-start | bytes 786440 | tf_op jit(solution)/shard_map/ppermute | solution.py:440
  48.8 5.2 %collective-permute-start.9 = (f32[12,8,256]{2,1,0:T(8,128)S(1)}, f32[12,8,256]{2,1,0:T(8,128)S(1)}, u32[]{:S(2)}, u32[]{:S(2)}) collective-permute-start(f32[12,8,256]{2,1,0:T(8,128)S(1)} %get-tuple-element.68), channel_id=1, source_target_pairs={{0,4},{4,0},{8,12},{12,8},{16,20},{20,16},{24,28},{28,24},{32,36},... | collective-permute-start | bytes 294920 | tf_op jit(solution)/shard_map/ppermute | solution.py:440
  48.9 13.4 %collective-permute-start.11 = (f32[12,8,256]{2,1,0:T(8,128)S(1)}, f32[12,8,256]{2,1,0:T(8,128)S(1)}, u32[]{:S(2)}, u32[]{:S(2)}) collective-permute-start(f32[12,8,256]{2,1,0:T(8,128)S(1)} %get-tuple-element.72), channel_id=1, source_target_pairs={{4,8},{8,4},{12,16},{16,12},{20,24},{24,20},{28,32},{32,28},{36,40... | collective-permute-start | bytes 294920 | tf_op jit(solution)/shard_map/ppermute | solution.py:440
  68.3 1.3 %collective-permute-start.12 = (f32[8,128]{1,0:T(8,128)S(1)}, f32[8,128]{1,0:T(8,128)S(1)}, u32[]{:S(2)}, u32[]{:S(2)}) collective-permute-start(f32[8,128]{1,0:T(8,128)S(1)} %get-tuple-element.76), channel_id=1, source_target_pairs={{0,4},{4,0},{8,12},{12,8},{16,20},{20,16},{24,28},{28,24},{32,36},... | collective-permute-start | bytes 12296 | tf_op jit(solution)/shard_map/ppermute | solution.py:486

commit v2 on v1

--- a/solution.py
+++ b/solution.py
@@ -14,7 +14,9 @@
 F32 = jnp.float32
 H = 4
 COEFS = 4
-GROUPS = (4, 4)
+CHUNK = 4
+INNER_ROWS = (6, 7, 13, 12)
+FAR_ROWS = (19, 12, 17, 16)
 PAD = 8
 
 C_FROM, D_FROM, A_FROM, B_FROM = range(4)
@@ -102,10 +104,9 @@
         ke_ref[H + z, pl.ds(PAD + H, ny), :] = k_turned[z * ny : (z + 1) * ny]
     for copy in copies:
         copy.wait()
-
-    for z in range(0, nz, 4):
-        block = p_ref.at[pl.ds(H + z, 4), pl.ds(H, ny)]
-        block[...] = permuted(block[...].reshape(4 * ny * vectors, nx), matrix).reshape(4, ny, vectors, nx)
+    for z in range(0, nz, CHUNK):
+        block = p_ref.at[pl.ds(H + z, CHUNK), pl.ds(H, ny)]
+        block[...] = permuted(block[...].reshape(CHUNK * ny * vectors, nx), matrix).reshape(CHUNK, ny, vectors, nx)
     cut_faces(where, p_ref, faces, nz=nz, ny=ny)
     c_low = where[C_FROM] == 0
     for z in range(nz):
@@ -162,7 +163,7 @@
                 out_ref[len(CORNER) + n // 8, pl.ds(n % 8, 1), :] = row
 
 
-def fill_side(where, side, p_ref, ke_ref, face_ref, corner_ref, *, nz, ny):
+def fill_face(where, side, p_ref, ke_ref, face_ref, *, nz, ny):
     start = where[A_TO + side]
 
     def row(y, _):
@@ -171,18 +172,22 @@
         return 0
 
     lax.fori_loop(0, ny, row, 0, unroll=4)
-    for n, (dz, dy, high) in enumerate(CORNER):
-        p_ref[halo_layer(where, side, dz, nz), halo_row(dy, high, ny)] = corner_ref[n]
     if ke_ref is not None:
         for z in range(H):
             for g in range(ny // 8):
                 ke_ref[start + z, pl.ds(PAD + H + 8 * g, 8), :] = face_ref[H * ny + z * (ny // 8) + g]
+
+
+def fill_corner(where, side, p_ref, ke_ref, corner_ref, *, nz, ny):
+    for n, (dz, dy, high) in enumerate(CORNER):
+        p_ref[halo_layer(where, side, dz, nz), halo_row(dy, high, ny)] = corner_ref[n]
+    if ke_ref is not None:
         for n, (dz, dy, high) in enumerate(CORNER):
             row = corner_ref[len(CORNER) + n // 8, pl.ds(n % 8, 1), :]
             ke_ref[halo_layer(where, side, dz, nz), pl.ds(PAD + halo_row(dy, high, ny), 1), :] = row
 
 
-def coefficients(ke_ref, coef, z0, count):
+def coefficients(ke_ref, coef, z0, count, groups=None):
     diag_ref, wz_ref, wy_ref, wx_ref = coef
     deep, wide = diag_ref.shape[0], diag_ref.shape[1]
     lane = lanes()
@@ -190,7 +195,7 @@
     def one(i, _):
         z = z0 + i
         below, above = jnp.maximum(z - 1, 0), jnp.minimum(z + 1, deep - 1)
-        for g in range(wide // 8):
+        for g in range(wide // 8) if groups is None else groups:
             at = PAD + 8 * g
             rows = pl.ds(8 * g, 8)
             k = ke_ref[z, pl.ds(at, 8), :]
@@ -227,49 +232,40 @@
             (even, odd), (inner, outer) = value, weights
             return inner * odd + pltpu.roll(outer * odd, 1, 1), inner * even + outer * pltpu.roll(even, 127, 1)
 
-        def fetch(n):
-            z = z0 + n
-            return dict(
-                ends=(field(z, y - 1), field(z, y + group)),
-                wy=[weight(wy_ref, z, y - 1 + r) for r in range(group + 1)],
-                diag=[weight(diag_ref, z, y + r) for r in range(group)],
-                old=None if first else [[old_ref[z, y + r, :, part] for part in both] for r in range(group)],
-            )
-
         below = [field(z0 - 1, y + r) for r in range(group)]
         here = [field(z0, y + r) for r in range(group)]
         wbelow = [weight(wz_ref, z0 - 1, y + r) for r in range(group)]
-        sides = [across(here[r], weight(wx_ref, z0, y + r)) for r in range(group)]
-        got = fetch(0)
         for n in range(zcount):
             z = z0 + n
-            above = [field(z + 1, y + r) for r in range(group)]
-            wabove = [weight(wz_ref, z, y + r) for r in range(group)]
-            column = [got["ends"][0], *here, got["ends"][1]]
-            made = []
+            above, wabove = [], []
+            south, wsouth = field(z, y - 1), weight(wy_ref, z, y - 1)
             for r in range(group):
+                north = here[r + 1] if r + 1 < group else field(z, y + group)
+                above.append(field(z + 1, y + r))
+                wabove.append(weight(wz_ref, z, y + r))
+                wnorth, diag = weight(wy_ref, z, y + r), weight(diag_ref, z, y + r)
+                sides = across(here[r], weight(wx_ref, z, y + r))
                 for part in range(2):
                     pulled = wabove[r][part] * above[r][part] + wbelow[r][part] * below[r][part]
-                    pulled += got["wy"][r + 1][part] * column[r + 2][part] + got["wy"][r][part] * column[r][part]
-                    image = got["diag"][r][part] * here[r][part] - (pulled + sides[r][part])
-                    made.append((r, part, 0.5 * image if first else image - got["old"][r][part]))
-            if n + 1 < zcount:
-                sides = [across(above[r], weight(wx_ref, z + 1, y + r)) for r in range(group)]
-                got = fetch(n + 1)
-            for r, part, value in made:
-                store(z, y + r, part, value)
+                    pulled += wnorth[part] * north[part] + wsouth[part] * south[part]
+                    image = diag[part] * here[r][part] - (pulled + sides[part])
+                    store(z, y + r, part, 0.5 * image if first else image - old_ref[z, y + r, :, both[part]])
+                south, wsouth = here[r], wnorth
             below, here, wbelow = here, above, wabove
 
     def many(i, _):
         rows(y0 + group * i, group)
         return 0
 
-    lax.fori_loop(0, ycount // group, many, 0)
-    if ycount % group:
+    if ycount > group:
+        lax.fori_loop(0, ycount // group, many, 0)
+    else:
+        rows(y0, ycount)
+    if ycount > group and ycount % group:
         rows(y0 + ycount - ycount % group, ycount % group)
 
 
-def steps(where, side, coef, p_ref, q_ref, last_store, *, nz, ny):
+def steps(where, region, coef, p_ref, q_ref, last_store, *, nz, ny):
     def into(ref):
         def store(z, y, part, value):
             ref[z, y, :, pl.ds(128 * part, 128)] = value
@@ -281,28 +277,55 @@
         h = H - step
         now, old = (p_ref, q_ref) if step % 2 == 1 else (q_ref, p_ref)
         store = last_store if step == H and last_store is not None else into(old)
-        if side == 0:
+        if region == "far":
+            z0, zcount = jnp.where(odd, H + nz - step, H - h), h + step
+        else:
             z0, zcount = jnp.where(odd, H - h, H + step), nz + h - step
+        if region == "far":
+            stretches = [(H - h, ny + 2 * h, FAR_ROWS[step - 1])]
+        elif region == "inner":
+            stretches = [(H + step, ny - 2 * step, INNER_ROWS[step - 1])]
         else:
-            z0, zcount = jnp.where(odd, H + nz - step, H - h), h + step
-        sweep(coef, now, old, store, z0, zcount, H - h, ny + 2 * h, step == 1, GROUPS[side])
-
-
-def near_kernel(where, p_in, *rest, nz, ny, first):
+            stretches = [(H - h, h + step, H), (H + ny - step, h + step, H)]
+        for y0, ycount, group in stretches:
+            sweep(coef, now, old, store, z0, zcount, y0, ycount, step == 1, group)
+
+
+def near_layers(where):
+    return jnp.where(where[Z_ODD] == 1, 0, H)
+
+
+def inner_kernel(where, p_in, *rest, nz, ny, first):
     size = dict(nz=nz, ny=ny)
     if first:
-        ke_in, face_ref, corner_ref, p_ref, ke_ref, q_ref, *coef = rest
+        ke_in, face_ref, p_ref, ke_ref, q_ref, *coef = rest
         store = None
     else:
-        *coef, face_ref, corner_ref, p_ref, q_ref, left_ref, right_ref, g_ref = rest
+        *coef, face_ref, p_ref, q_ref, even_ref, odd_ref = rest
         ke_ref = None
-        store = filtered_store((left_ref, right_ref), **size)
-    fill_side(where, 0, p_ref, ke_ref, face_ref, corner_ref, **size)
-    if first:
-        coefficients(ke_ref, coef, jnp.where(where[Z_ODD] == 1, 0, H), nz + H)
-    steps(where, 0, coef, p_ref, q_ref, store, **size)
+        store = filtered_store((even_ref, odd_ref), **size)
+    fill_face(where, 0, p_ref, ke_ref, face_ref, **size)
+    if first:
+        coefficients(ke_ref, coef, near_layers(where), nz + H)
+    steps(where, "inner", coef, p_ref, q_ref, store, **size)
+
+
+def edges_kernel(where, p_in, q_in, *rest, nz, ny, first):
+    size = dict(nz=nz, ny=ny)
+    if first:
+        ke_in, *rest = rest
+        corner_ref, p_ref, q_ref, ke_ref, *coef = rest[COEFS:]
+        store = None
+    else:
+        *coef, corner_ref, even_in, odd_in, p_ref, q_ref, even_ref, odd_ref, g_ref = rest
+        ke_ref = None
+        store = filtered_store((even_ref, odd_ref), **size)
+    fill_corner(where, 0, p_ref, ke_ref, corner_ref, **size)
+    if first:
+        coefficients(ke_ref, coef, near_layers(where), nz + H, groups=(0, (ny + 2 * H) // 8 - 1))
+    steps(where, "edges", coef, p_ref, q_ref, store, **size)
     if not first:
-        pairs = products((left_ref, right_ref), where[A_FROM] * ny // 8, H * ny // 8, nz * ny, None)
+        pairs = products((even_ref, odd_ref), where[A_FROM] * ny // 8, H * ny // 8, nz * ny, None)
         for n, total in enumerate(pairs):
             g_ref[n] = total
 
@@ -311,22 +334,22 @@
     size = dict(nz=nz, ny=ny)
     if first:
         ke_in, *rest = rest
-        rest = rest[COEFS:]
-        face_ref, corner_ref, p_ref, q_ref, ke_ref, *rest = rest
+        face_ref, corner_ref, p_ref, q_ref, ke_ref, *rest = rest[COEFS:]
         coef, faces = rest[:COEFS], rest[COEFS:]
         store = None
     else:
-        *coef, face_ref, corner_ref, left_in, right_in, pairs_ref, p_ref, q_ref, left_ref, right_ref, g_ref = rest
+        *coef, face_ref, corner_ref, even_in, odd_in, pairs_ref, p_ref, q_ref, even_ref, odd_ref, g_ref = rest
         ke_ref = None
-        store = filtered_store((left_ref, right_ref), **size)
-    fill_side(where, 1, p_ref, ke_ref, face_ref, corner_ref, **size)
+        store = filtered_store((even_ref, odd_ref), **size)
+    fill_face(where, 1, p_ref, ke_ref, face_ref, **size)
+    fill_corner(where, 1, p_ref, ke_ref, corner_ref, **size)
     if first:
         coefficients(ke_ref, coef, jnp.where(where[Z_ODD] == 1, H + nz - 1, 0), H + 1)
-    steps(where, 1, coef, p_ref, q_ref, store, **size)
+    steps(where, "far", coef, p_ref, q_ref, store, **size)
     if first:
         cut_faces(where, p_ref, faces, **size)
     else:
-        sums = products((left_ref, right_ref), where[B_FROM] * ny // 8, H * ny // 8, nz * ny, pairs_ref)
+        sums = products((even_ref, odd_ref), where[B_FROM] * ny // 8, H * ny // 8, nz * ny, pairs_ref)
         row_of = lax.broadcasted_iota(jnp.int32, g_ref.shape, 0)
         col_of = lax.broadcasted_iota(jnp.int32, g_ref.shape, 1)
         gram = jnp.zeros(g_ref.shape, F32)
@@ -359,62 +382,63 @@
     return lax.fori_loop(0, count, group, tuple(zero))
 
 
-def basis_kernel(g_ref, even_ref, odd_ref, out_ref, w_ref, made_ref, *, scale):
-    vectors = out_ref.shape[0]
-
-    @pl.when(pl.program_id(0) == 0)
-    def _():
-        row = lax.broadcasted_iota(jnp.int32, (vectors, 128), 0)
-        col = lax.broadcasted_iota(jnp.int32, (vectors, 128), 1)
-        gram = jnp.sum(g_ref[...], axis=0)
-        both = jnp.where(col < vectors, gram, jnp.where(col - vectors == row, 1.0, 0.0))
-        scales = jnp.zeros((vectors, 128), F32)
-        for k in range(vectors):
-            pivot_row = jnp.broadcast_to(both[k : k + 1, :], both.shape)
-            pivot = jnp.broadcast_to(pivot_row[:, k : k + 1], both.shape)
-            scales = jnp.where(row == k, scale * lax.rsqrt(pivot), scales)
-            if k + 1 < vectors:
-                factor = jnp.broadcast_to(both[:, k : k + 1], both.shape) / pivot
-                both = both - jnp.where(row > k, factor, 0.0) * pivot_row
-        w_ref[...] = both * scales
-
-    have = w_ref[...]
-    spread = lambda v, w: jnp.broadcast_to(have[v : v + 1, vectors + w : vectors + w + 1], (8, 128))
+def basis_kernel(g_ref, even_ref, odd_ref, out_ref, made_ref, ready_ref, sems, *, scale, blocks):
+    vectors, cells = made_ref.shape[0], made_ref.shape[1]
+    row = lax.broadcasted_iota(jnp.int32, (vectors, 128), 0)
+    col = lax.broadcasted_iota(jnp.int32, (vectors, 128), 1)
+    gram = jnp.sum(g_ref[...], axis=0)
+    both = jnp.where(col < vectors, gram, jnp.where(col - vectors == row, 1.0, 0.0))
+    scales = jnp.zeros((vectors, 128), F32)
+    for k in range(vectors):
+        pivot_row = jnp.broadcast_to(both[k : k + 1, :], both.shape)
+        pivot = jnp.broadcast_to(pivot_row[:, k : k + 1], both.shape)
+        scales = jnp.where(row == k, scale * lax.rsqrt(pivot), scales)
+        if k + 1 < vectors:
+            factor = jnp.broadcast_to(both[:, k : k + 1], both.shape) / pivot
+            both = both - jnp.where(row > k, factor, 0.0) * pivot_row
+    both = both * scales
+    spread = lambda v, w: jnp.broadcast_to(both[v : v + 1, vectors + w : vectors + w + 1], (8, 128))
     weights = [[spread(v, w) for w in range(v + 1)] for v in range(vectors)]
-    count = out_ref.shape[1]
-    first = pl.program_id(0) * count
-
-    def combine(i, _):
-        for part, ref in enumerate((even_ref, odd_ref)):
-            field = [ref[v, pl.ds(pl.multiple_of(first + i * 8, 8), 8), :] for v in range(vectors)]
-            for v in range(vectors):
-                total = weights[v][0] * field[0]
-                for w in range(1, v + 1):
-                    total = total + weights[v][w] * field[w]
-                made_ref[v, pl.ds(pl.multiple_of(i * 8, 8), 8), pl.ds(part * 128, 128)] = total
-        return 0
-
-    lax.fori_loop(0, count // 8, combine, 0)
     matrix = even_first(back=True)
-
-    made = permuted(made_ref[...].reshape(vectors * count, 256), matrix, terms=2)
-    out_ref[...] = made.reshape(out_ref.shape)
-
-
-def basis(gram, left, right, cells, scale):
+    count = cells // blocks
+    copies = []
+    for block in range(blocks):
+        first = block * count
+
+        def combine(i, _, first=first):
+            at = pl.ds(pl.multiple_of(first + i * 8, 8), 8)
+            for part, ref in enumerate((even_ref, odd_ref)):
+                field = [ref[v, at, :] for v in range(vectors)]
+                for v in range(vectors):
+                    total = weights[v][0] * field[0]
+                    for w in range(1, v + 1):
+                        total = total + weights[v][w] * field[w]
+                    made_ref[v, at, pl.ds(part * 128, 128)] = total
+            return 0
+
+        lax.fori_loop(0, count // 8, combine, 0, unroll=2)
+        rows = pl.ds(first, count)
+        made = permuted(made_ref[:, rows, :].reshape(vectors * count, 256), matrix, terms=2)
+        ready_ref[:, rows, :] = made.reshape(vectors, count, 256)
+        copies.append(pltpu.make_async_copy(ready_ref.at[:, rows, :], out_ref.at[:, rows, :], sems.at[block]))
+        copies[-1].start()
+    for copy in copies:
+        copy.wait()
+
+
+def basis(gram, even, odd, cells, scale):
     vectors = gram.shape[1]
-    blocks = 4
-    rows = cells // blocks
+    blocks = 2
+    shape = (vectors, cells, 256)
     return pl.pallas_call(
-        functools.partial(basis_kernel, scale=scale),
-        grid=(blocks,),
-        out_shape=jax.ShapeDtypeStruct((vectors, cells, 256), F32),
+        functools.partial(basis_kernel, scale=scale, blocks=blocks),
+        out_shape=jax.ShapeDtypeStruct(shape, F32),
         in_specs=[pl.BlockSpec(memory_space=pltpu.VMEM)] * 3,
-        out_specs=pl.BlockSpec((vectors, rows, 256), lambda i: (0, i, 0)),
-        scratch_shapes=[pltpu.VMEM((vectors, 128), F32), pltpu.VMEM((vectors, rows, 256), F32)],
+        out_specs=pl.BlockSpec(memory_space=pltpu.HBM),
+        scratch_shapes=[pltpu.VMEM(shape, F32), pltpu.VMEM(shape, F32), pltpu.SemaphoreType.DMA((blocks,))],
         compiler_params=pltpu.CompilerParams(vmem_limit_bytes=16 << 20),
         name="basis",
-    )(gram, left.reshape(vectors, cells, 128), right.reshape(vectors, cells, 128))
+    )(gram, even.reshape(vectors, cells, 128), odd.reshape(vectors, cells, 128))
 
 
 def shards(block, conduct):
@@ -439,44 +463,55 @@
     kernel = lambda f, **more: functools.partial(f, nz=nz, ny=ny, **more)
     swap = lambda payload, pairs: lax.ppermute(payload, *pairs)
 
-    def exchange(p, ke, a, b, c, d):
+    def begin(a, b, c, d):
         c = swap(c, c_pairs)
         d = swap(d, d_pairs)
+        a = swap(a, a_pairs)
         b = swap(b, b_pairs)
-        a = swap(a, a_pairs)
+        return a, b, c, d
+
+    def corners(p, ke, c, d):
         first = ke is not None
         n = corner + 2 if first else corner
         keep = [field] + ([ke.shape] if first else [])
-        outs = keep + [(n, *row)] * 2
         args = (where, p) + ((ke,) if first else ()) + (c, d)
         alias = {1: 0, 2: 1} if first else {1: 0}
-        *kept, ac, bc = call(kernel(corner_kernel, first=first), outs, args, alias)
+        *kept, ac, bc = call(kernel(corner_kernel, first=first), keep + [(n, *row)] * 2, args, alias)
         ac = swap(ac, a_pairs)
         bc = swap(bc, b_pairs)
-        return kept, a, b, ac, bc
-
-    near_flops, far_flops = 20_000_000, 12_000_000
+        return kept, ac, bc
+
+    inner_flops, edge_flops, far_flops = 16_000_000, 4_000_000, 12_000_000
     extra_z, extra_y = H * ny // 8, nz * H // 8
     p, k, a, b, c, d = call(
         kernel(turn_kernel),
         [field, ke, (H * ny + extra_z, *row), (H * ny + extra_z, *row), (nz * H + extra_y, *row), (nz * H + extra_y, *row)],
         (where, *(pltpu.with_memory_space_constraint(arg, pltpu.HBM) for arg in (block, conduct))), space=pltpu.HBM,
         scratch=[pltpu.VMEM(conduct.shape, F32), pltpu.SemaphoreType.DMA((vectors,)), pltpu.SemaphoreType.DMA])
-    (p, k), a, b, ac, bc = exchange(p, k, a, b, c, d)
-    p, k, q, *coef = call(kernel(near_kernel, first=True), [field, ke, field, *weights], (where, p, k, a, ac),
-                          {1: 0, 2: 1}, flops=near_flops)
+    a, b, c, d = begin(a, b, c, d)
+    p, k, q, *coef = call(kernel(inner_kernel, first=True), [field, ke, field, *weights], (where, p, k, a),
+                          {1: 0, 2: 1}, flops=inner_flops)
+    (p, k), ac, bc = corners(p, k, c, d)
+    p, q, k, *coef = call(
+        kernel(edges_kernel, first=True), [field, field, ke, *weights], (where, p, q, k, *coef, ac),
+        {n + 1: n for n in range(3 + COEFS)}, flops=edge_flops)
     p, q, k, *rest = call(
         kernel(far_kernel, first=True),
         [field, field, ke, *weights, (H * ny, *row), (H * ny, *row), (nz * H, *row), (nz * H, *row)],
         (where, p, q, k, *coef, b, bc), {n + 1: n for n in range(3 + COEFS)}, flops=far_flops)
     coef, (a, b, c, d) = rest[:COEFS], rest[COEFS:]
-    (p,), a, b, ac, bc = exchange(p, None, a, b, c, d)
+    a, b, c, d = begin(a, b, c, d)
+    p, q, left, right = call(kernel(inner_kernel, first=False), [field, field, *halves_shape], (where, p, *coef, a),
+                             {1: 0}, flops=inner_flops)
+    (p,), ac, bc = corners(p, None, c, d)
     p, q, left, right, pairs = call(
-        kernel(near_kernel, first=False), [field, field, *halves_shape, (len(PAIRS), 8, 128)],
-        (where, p, *coef, a, ac), {1: 0}, flops=near_flops)
+        kernel(edges_kernel, first=False), [field, field, *halves_shape, (len(PAIRS), 8, 128)],
+        (where, p, q, *coef, ac, left, right), {1: 0, 2: 1, COEFS + 4: 2, COEFS + 5: 3},
+        flops=edge_flops)
     _, _, left, right, gram = call(
         kernel(far_kernel, first=False), [field, field, *halves_shape, (vectors, 128)],
-        (where, p, q, *coef, b, bc, left, right, pairs), {1: 0, 2: 1, COEFS + 5: 2, COEFS + 6: 3}, flops=far_flops)
+        (where, p, q, *coef, b, bc, left, right, pairs), {1: 0, 2: 1, COEFS + 5: 2, COEFS + 6: 3},
+        flops=far_flops)
     gram = sum_everywhere(gram, zcount, ycount)
     out = basis(gram, left, right, cells, math.sqrt(nx * cells * zcount * ycount))
     return out.reshape(block.shape)

time: 105 us -> 94.2 us (0.90)
  waiting for transfers between devices: 11.7 us -> 1.74 us
    ppermute x12, waiting for transfers between devices: 10.5 us -> 0.58 us  [shards(): swap = lambda payload, pairs: lax.ppermute(payload, *pairs)]
    pallas_call x7 -> x9, Pallas kernels: 32.8 us -> 32.6 us  [call(): pl.pallas_call(kernel, out_shape=[jax.ShapeDtypeStruct(s, F32) for s in o...]
  transfers between devices with their start and end apart: 13 -> 13, of which waited for: 3 -> 2; matrix products, arithmetic and copies ran while one was open for 0% -> 0% of each run, Pallas kernels for 17% -> 20%
where the time goes in v2:
time: 94.2 us; the launch traced here: 93.2 us
  Pallas kernels  36.7 us (39%)
  blocking collectives  30.3 us (32%)
  starting transfers between devices  24.1 us (26%)
  waiting for transfers between devices  1.74 us (2%)
    pallas_call x9, Pallas kernels, call(): pl.pallas_call(kernel, out_shape=[jax.ShapeDtypeStruct(s, F32) for s in o...  32.6 us
    all_to_all x2, blocking collectives, gathered(): lax.all_to_all(copies, axes, 0, 0, axis_index_groups=groups, tiled=True)  30.3 us
    ppermute x12, starting transfers between devices, shards(): swap = lambda payload, pairs: lax.ppermute(payload, *pairs)  24 us
    pallas_call x1, Pallas kernels, basis(): pl.pallas_call(functools.partial(basis_kernel, scale=scale, blocks=blocks...  4.08 us
  transfers between devices with their start and end apart: 13, of which 2 were waited for; matrix products, arithmetic and copies ran while one was open for 0% of the time, Pallas kernels for 20%

profile of v2, /device:TPU:1, one launch (start us, length us, event | category | flops | bytes accessed | tf_op | source)
XLA Modules:
  0.0 93.2 jit_solution(67453115824295754)
XLA Ops:
  0.0 0.1 stack.39.where
  0.1 3.7 %shard_map.28 = (f32[16,40,8,256]{3,2,1,0:T(8,128)S(1)}, f32[16,56,256]{2,1,0:T(8,128)S(1)}, f32[144,8,256]{2,1,0:T(8,128)S(1)}, f32[144,8,256]{2,1,0:T(8,128)S(...) custom-call(s32[9]{0:T(128)S(1)} %stack.39.where, f32[8,8,32,256]{3,2,1,0:T(8,128)} %x_ref.1, f32[8,32,256]{2,1,0:T(8,128)} %k_ref.1), custom_call_target="tpu_custom_call" | custom-call | bytes 65536 | tf_op jit(solution)/shard_map/pallas_call | solution.py:32
  3.8 3.3 %collective-permute-start = (f32[144,8,256]{2,1,0:T(8,128)S(1)}, f32[144,8,256]{2,1,0:T(8,128)S(1)}, u32[]{:S(2)}, u32[]{:S(2)}) collective-permute-start(f32[144,8,256]{2,1,0:T(8,128)S(1)} %get-tuple-element.55), channel_id=1, source_target_pairs={{0,4},{4,0},{8,12},{12,8},{16,20},{20,16},{24,28},{28,24},{32,36},... | collective-permute-start | bytes 3538952 | tf_op jit(solution)/shard_map/ppermute | solution.py:464
  7.1 1.9 %collective-permute-start.4 = (f32[144,8,256]{2,1,0:T(8,128)S(1)}, f32[144,8,256]{2,1,0:T(8,128)S(1)}, u32[]{:S(2)}, u32[]{:S(2)}) collective-permute-start(f32[144,8,256]{2,1,0:T(8,128)S(1)} %get-tuple-element.75), channel_id=1, source_target_pairs={{4,8},{8,4},{12,16},{16,12},{20,24},{24,20},{28,32},{32,28},{36,40... | collective-permute-start | bytes 3538952 | tf_op jit(solution)/shard_map/ppermute | solution.py:464
  9.0 1.1 %collective-permute-start.1 = (f32[36,8,256]{2,1,0:T(8,128)S(1)}, f32[36,8,256]{2,1,0:T(8,128)S(1)}, u32[]{:S(2)}, u32[]{:S(2)}) collective-permute-start(f32[36,8,256]{2,1,0:T(8,128)S(1)} %get-tuple-element.58), channel_id=1, source_target_pairs={{0,1},{1,0},{2,3},{3,2},{4,5},{5,4},{6,7},{7,6},{8,9},{9,8},{10,11... | collective-permute-start | bytes 884744 | tf_op jit(solution)/shard_map/ppermute | solution.py:464
  10.1 0.7 collective-permute-start.2
  10.8 0.0 collective-permute-done.rest_1_
  10.8 6.3 %shard_map.29 = (f32[16,40,8,256]{3,2,1,0:T(8,128)S(1)}, f32[16,56,256]{2,1,0:T(8,128)S(1)}, f32[16,40,8,256]{3,2,1,0:T(8,128)S(1)}, f32[16,40,256]{2,1,0:T(8,12...) custom-call(s32[9]{0:T(128)S(1)} %stack.39.where, ...), custom_call_target="tpu_custom_call", output_to_operand_aliasing={{0}: (1, {}), {1}: (2, {})} | custom-call | flops 16000000 | bytes 65536 | tf_op jit(solution)/shard_map/pallas_call | solution.py:32
  17.1 0.0 collective-permute-done.1.rest_1_
  17.1 0.0 collective-permute-done.2.rest_2_
  17.1 0.6 shard_map.30
  17.8 0.1 collective-permute-start.3
  17.9 4.6 %collective-permute-start.5 = (f32[14,8,256]{2,1,0:T(8,128)S(1)}, f32[14,8,256]{2,1,0:T(8,128)S(1)}, u32[]{:S(2)}, u32[]{:S(2)}) collective-permute-start(f32[14,8,256]{2,1,0:T(8,128)S(1)} %get-tuple-element.76), channel_id=1, source_target_pairs={{4,8},{8,4},{12,16},{16,12},{20,24},{24,20},{28,32},{32,28},{36,40... | collective-permute-start | bytes 344072 | tf_op jit(solution)/shard_map/ppermute | solution.py:464
  22.5 0.0 collective-permute-done.3.rest_5_
  22.5 2.7 %shard_map.31 = (f32[16,40,8,256]{3,2,1,0:T(8,128)S(1)}, f32[16,40,8,256]{3,2,1,0:T(8,128)S(1)}, f32[16,56,256]{2,1,0:T(8,128)S(1)}, f32[16,40,256]{2,1,0:T(8,12...) custom-call(s32[9]{0:T(128)S(1)} %stack.39.where, ...), custom_call_target="tpu_custom_call", output_to_operand_aliasing={{0}: (1, {}), {1}: (2, {}), {2}: (3, {}), {3}: (4, {}), {4}... | custom-call | flops 4000000 | bytes 65536 | tf_op jit(solution)/shard_map/pallas_call | solution.py:32
  25.2 0.0 collective-permute-done.4.rest_5_
  25.3 0.5 collective-permute-done.5.rest_6_
  25.8 5.0 %shard_map.32 = (f32[16,40,8,256]{3,2,1,0:T(8,128)S(1)}, f32[16,40,8,256]{3,2,1,0:T(8,128)S(1)}, f32[16,56,256]{2,1,0:T(8,128)S(1)}, f32[16,40,256]{2,1,0:T(8,12...) custom-call(s32[9]{0:T(128)S(1)} %stack.39.where, ...), custom_call_target="tpu_custom_call", output_to_operand_aliasing={{0}: (1, {}), {1}: (2, {}), {2}: (3, {}), {3}: (4, {}), {4}... | custom-call | flops 12000000 | bytes 65536 | tf_op jit(solution)/shard_map/pallas_call | solution.py:32
  30.8 0.1 collective-permute-start.6
  30.9 3.3 %collective-permute-start.10 = (f32[128,8,256]{2,1,0:T(8,128)S(1)}, f32[128,8,256]{2,1,0:T(8,128)S(1)}, u32[]{:S(2)}, u32[]{:S(2)}) collective-permute-start(f32[128,8,256]{2,1,0:T(8,128)S(1)} %get-tuple-element.93), channel_id=1, source_target_pairs={{4,8},{8,4},{12,16},{16,12},{20,24},{24,20},{28,32},{32,28},{36,40... | collective-permute-start | bytes 3145736 | tf_op jit(solution)/shard_map/ppermute | solution.py:464
  34.2 3.9 %collective-permute-start.7 = (f32[32,8,256]{2,1,0:T(8,128)S(1)}, f32[32,8,256]{2,1,0:T(8,128)S(1)}, u32[]{:S(2)}, u32[]{:S(2)}) collective-permute-start(f32[32,8,256]{2,1,0:T(8,128)S(1)} %get-tuple-element.84), channel_id=1, source_target_pairs={{0,1},{1,0},{2,3},{3,2},{4,5},{5,4},{6,7},{7,6},{8,9},{9,8},{10,11... | collective-permute-start | bytes 786440 | tf_op jit(solution)/shard_map/ppermute | solution.py:464
  38.0 0.7 collective-permute-start.8
  38.7 0.0 collective-permute-done.6.rest_4_
  38.7 5.7 %shard_map.33 = (f32[16,40,8,256]{3,2,1,0:T(8,128)S(1)}, f32[16,40,8,256]{3,2,1,0:T(8,128)S(1)}, f32[2048,128]{1,0:T(8,128)S(1)}, f32[2048,128]{1,0:T(8,128)S(1)}) custom-call(s32[9]{0:T(128)S(1)} %stack.39.where, f32[16,40,8,256]{3,2,1,0:T(8,128)S(1)} %get-tuple-element.77.p_in, ...), custom_call_target="tpu_custom_call", output_to_operand_aliasing={{0}: (1, {})} | custom-call | flops 16000000 | bytes 65536 | tf_op jit(solution)/shard_map/pallas_call | solution.py:32
  44.4 0.0 collective-permute-done.7.rest_0_
  44.4 0.0 collective-permute-done.8.rest_1_
  44.5 0.6 shard_map.34
  45.1 0.1 collective-permute-start.9
  45.2 4.3 %collective-permute-start.11 = (f32[12,8,256]{2,1,0:T(8,128)S(1)}, f32[12,8,256]{2,1,0:T(8,128)S(1)}, u32[]{:S(2)}, u32[]{:S(2)}) collective-permute-start(f32[12,8,256]{2,1,0:T(8,128)S(1)} %get-tuple-element.94), channel_id=1, source_target_pairs={{4,8},{8,4},{12,16},{16,12},{20,24},{24,20},{28,32},{32,28},{36,40... | collective-permute-start | bytes 294920 | tf_op jit(solution)/shard_map/ppermute | solution.py:464
  49.5 0.0 collective-permute-done.9.rest_4_
  49.5 2.4 %shard_map.35 = (f32[16,40,8,256]{3,2,1,0:T(8,128)S(1)}, f32[16,40,8,256]{3,2,1,0:T(8,128)S(1)}, f32[2048,128]{1,0:T(8,128)S(1)}, f32[2048,128]{1,0:T(8,128)S(1)}, f32[36,8,128]{2,1,0:T(8,128)S(1)}) custom-call(s32[9]{0:T(128)S(1)} %stack.39.where, ...), custom_call_target="tpu_custom_call", output_to_operand_aliasing={{0}: (1, {}), {1}: (2, {}), {2}: (8, {}), {3}: (9, {})} | custom-call | flops 4000000 | bytes 65536 | tf_op jit(solution)/shard_map/pallas_call | solution.py:32
  51.9 0.0 collective-permute-done.10.rest_4_
  51.9 0.0 collective-permute-done.11.rest_5_
  51.9 5.5 %shard_map.36 = (f32[16,40,8,256]{3,2,1,0:T(8,128)S(1)}, f32[16,40,8,256]{3,2,1,0:T(8,128)S(1)}, f32[2048,128]{1,0:T(8,128)S(1)}, f32[2048,128]{1,0:T(8,128)S(1)}, f32[8,128]{1,0:T(8,128)S(1)}) custom-call(s32[9]{0:T(128)S(1)} %stack.39.where, ...), custom_call_target="tpu_custom_call", output_to_operand_aliasing={{0}: (1, {}), {1}: (2, {}), {2}: (9, {}), {3}: (10, {})} | custom-call | flops 12000000 | bytes 65536 | tf_op jit(solution)/shard_map/pallas_call | solution.py:32
  57.4 0.1 collective-permute-start.12
  57.5 1.2 %collective-permute-done.12 = f32[8,128]{1,0:T(8,128)S(1)} collective-permute-done((f32[8,128]{1,0:T(8,128)S(1)}, f32[8,128]{1,0:T(8,128)S(1)}, u32[]{:S(2)}, u32[]{:S(2)}) %collective-permute-start.12) | collective-permute-done | bytes 4128 | tf_op jit(solution)/shard_map/ppermute | solution.py:521
  58.7 19.5 %all_to_all.10 = f32[16,8,128]{2,1,0:T(8,128)S(1)} all-to-all(f32[16,8,128]{2,1,0:T(8,128)S(1)} %broadcast_in_dim.4), channel_id=1, replica_groups={{0,1,2,3,64,65,66,67,128,129,130,131,192,193,194,195},{4,5,6,7,68,69,70..., dimensions={0} | all-to-all | bytes 131072 | tf_op jit(solution)/shard_map/all_to_all | solution.py:537
  78.2 10.8 %all_to_all.11.g_ref = f32[8,8,128]{2,1,0:T(8,128)S(1)} all-to-all(f32[8,8,128]{2,1,0:T(8,128)S(1)} %broadcast_in_dim.5), channel_id=1, replica_groups={{0,8,16,24,32,40,48,56},{4,12,20,28,36,44,52,60},{64,72,80,88,96,104,11..., dimensions={0} | all-to-all | bytes 65536 | tf_op jit(solution)/shard_map/all_to_all | solution.py:537
  89.0 4.1 %basis.1 = f32[8,256,256]{2,1,0:T(8,128)} custom-call(f32[8,8,128]{2,1,0:T(8,128)S(1)} %all_to_all.11.g_ref, f32[8,256,128]{2,1,0:T(8,128)S(1)} %bitcast.12, f32[8,256,128]{2,1,0:T(8,128)S(1)} %bitcast.13), custom_call_target="tpu_custom_call" | custom-call | tf_op jit(solution)/shard_map/basis/pallas_call | solution.py:433
  (4 shorter events, 0.0 us)
Async XLA Ops:
  3.8 7.0 %collective-permute-start = (f32[144,8,256]{2,1,0:T(8,128)S(1)}, f32[144,8,256]{2,1,0:T(8,128)S(1)}, u32[]{:S(2)}, u32[]{:S(2)}) collective-permute-start(f32[144,8,256]{2,1,0:T(8,128)S(1)} %get-tuple-element.55), channel_id=1, source_target_pairs={{0,4},{4,0},{8,12},{12,8},{16,20},{20,16},{24,28},{28,24},{32,36},... | collective-permute-start | bytes 3538952 | tf_op jit(solution)/shard_map/ppermute | solution.py:464
  7.1 18.2 %collective-permute-start.4 = (f32[144,8,256]{2,1,0:T(8,128)S(1)}, f32[144,8,256]{2,1,0:T(8,128)S(1)}, u32[]{:S(2)}, u32[]{:S(2)}) collective-permute-start(f32[144,8,256]{2,1,0:T(8,128)S(1)} %get-tuple-element.75), channel_id=1, source_target_pairs={{4,8},{8,4},{12,16},{16,12},{20,24},{24,20},{28,32},{32,28},{36,40... | collective-permute-start | bytes 3538952 | tf_op jit(solution)/shard_map/ppermute | solution.py:464
  9.0 8.1 %collective-permute-start.1 = (f32[36,8,256]{2,1,0:T(8,128)S(1)}, f32[36,8,256]{2,1,0:T(8,128)S(1)}, u32[]{:S(2)}, u32[]{:S(2)}) collective-permute-start(f32[36,8,256]{2,1,0:T(8,128)S(1)} %get-tuple-element.58), channel_id=1, source_target_pairs={{0,1},{1,0},{2,3},{3,2},{4,5},{5,4},{6,7},{7,6},{8,9},{9,8},{10,11... | collective-permute-start | bytes 884744 | tf_op jit(solution)/shard_map/ppermute | solution.py:464
  10.1 7.0 %collective-permute-start.2 = (f32[36,8,256]{2,1,0:T(8,128)S(1)}, f32[36,8,256]{2,1,0:T(8,128)S(1)}, u32[]{:S(2)}, u32[]{:S(2)}) collective-permute-start(f32[36,8,256]{2,1,0:T(8,128)S(1)} %get-tuple-element.59), channel_id=1, source_target_pairs={{1,2},{2,1},{5,6},{6,5},{9,10},{10,9},{13,14},{14,13},{17,18},{18,... | collective-permute-start | bytes 884744 | tf_op jit(solution)/shard_map/ppermute | solution.py:464
  17.8 4.8 %collective-permute-start.3 = (f32[14,8,256]{2,1,0:T(8,128)S(1)}, f32[14,8,256]{2,1,0:T(8,128)S(1)}, u32[]{:S(2)}, u32[]{:S(2)}) collective-permute-start(f32[14,8,256]{2,1,0:T(8,128)S(1)} %get-tuple-element.67), channel_id=1, source_target_pairs={{0,4},{4,0},{8,12},{12,8},{16,20},{20,16},{24,28},{28,24},{32,36},... | collective-permute-start | bytes 344072 | tf_op jit(solution)/shard_map/ppermute | solution.py:464
  17.9 7.9 %collective-permute-start.5 = (f32[14,8,256]{2,1,0:T(8,128)S(1)}, f32[14,8,256]{2,1,0:T(8,128)S(1)}, u32[]{:S(2)}, u32[]{:S(2)}) collective-permute-start(f32[14,8,256]{2,1,0:T(8,128)S(1)} %get-tuple-element.76), channel_id=1, source_target_pairs={{4,8},{8,4},{12,16},{16,12},{20,24},{24,20},{28,32},{32,28},{36,40... | collective-permute-start | bytes 344072 | tf_op jit(solution)/shard_map/ppermute | solution.py:464
  30.8 7.9 %collective-permute-start.6 = (f32[128,8,256]{2,1,0:T(8,128)S(1)}, f32[128,8,256]{2,1,0:T(8,128)S(1)}, u32[]{:S(2)}, u32[]{:S(2)}) collective-permute-start(f32[128,8,256]{2,1,0:T(8,128)S(1)} %get-tuple-element.82), channel_id=1, source_target_pairs={{0,4},{4,0},{8,12},{12,8},{16,20},{20,16},{24,28},{28,24},{32,36},... | collective-permute-start | bytes 3145736 | tf_op jit(solution)/shard_map/ppermute | solution.py:464
  30.9 21.0 %collective-permute-start.10 = (f32[128,8,256]{2,1,0:T(8,128)S(1)}, f32[128,8,256]{2,1,0:T(8,128)S(1)}, u32[]{:S(2)}, u32[]{:S(2)}) collective-permute-start(f32[128,8,256]{2,1,0:T(8,128)S(1)} %get-tuple-element.93), channel_id=1, source_target_pairs={{4,8},{8,4},{12,16},{16,12},{20,24},{24,20},{28,32},{32,28},{36,40... | collective-permute-start | bytes 3145736 | tf_op jit(solution)/shard_map/ppermute | solution.py:464
  34.2 10.2 %collective-permute-start.7 = (f32[32,8,256]{2,1,0:T(8,128)S(1)}, f32[32,8,256]{2,1,0:T(8,128)S(1)}, u32[]{:S(2)}, u32[]{:S(2)}) collective-permute-start(f32[32,8,256]{2,1,0:T(8,128)S(1)} %get-tuple-element.84), channel_id=1, source_target_pairs={{0,1},{1,0},{2,3},{3,2},{4,5},{5,4},{6,7},{7,6},{8,9},{9,8},{10,11... | collective-permute-start | bytes 786440 | tf_op jit(solution)/shard_map/ppermute | solution.py:464
  38.0 6.4 %collective-permute-start.8 = (f32[32,8,256]{2,1,0:T(8,128)S(1)}, f32[32,8,256]{2,1,0:T(8,128)S(1)}, u32[]{:S(2)}, u32[]{:S(2)}) collective-permute-start(f32[32,8,256]{2,1,0:T(8,128)S(1)} %get-tuple-element.85), channel_id=1, source_target_pairs={{1,2},{2,1},{5,6},{6,5},{9,10},{10,9},{13,14},{14,13},{17,18},{18,... | collective-permute-start | bytes 786440 | tf_op jit(solution)/shard_map/ppermute | solution.py:464
  45.1 4.4 %collective-permute-start.9 = (f32[12,8,256]{2,1,0:T(8,128)S(1)}, f32[12,8,256]{2,1,0:T(8,128)S(1)}, u32[]{:S(2)}, u32[]{:S(2)}) collective-permute-start(f32[12,8,256]{2,1,0:T(8,128)S(1)} %get-tuple-element.88), channel_id=1, source_target_pairs={{0,4},{4,0},{8,12},{12,8},{16,20},{20,16},{24,28},{28,24},{32,36},... | collective-permute-start | bytes 294920 | tf_op jit(solution)/shard_map/ppermute | solution.py:464
  45.2 6.7 %collective-permute-start.11 = (f32[12,8,256]{2,1,0:T(8,128)S(1)}, f32[12,8,256]{2,1,0:T(8,128)S(1)}, u32[]{:S(2)}, u32[]{:S(2)}) collective-permute-start(f32[12,8,256]{2,1,0:T(8,128)S(1)} %get-tuple-element.94), channel_id=1, source_target_pairs={{4,8},{8,4},{12,16},{16,12},{20,24},{24,20},{28,32},{32,28},{36,40... | collective-permute-start | bytes 294920 | tf_op jit(solution)/shard_map/ppermute | solution.py:464
  57.4 1.3 %collective-permute-start.12 = (f32[8,128]{1,0:T(8,128)S(1)}, f32[8,128]{1,0:T(8,128)S(1)}, u32[]{:S(2)}, u32[]{:S(2)}) collective-permute-start(f32[8,128]{1,0:T(8,128)S(1)} %get-tuple-element.98), channel_id=1, source_target_pairs={{0,4},{4,0},{8,12},{12,8},{16,20},{20,16},{24,28},{28,24},{32,36},... | collective-permute-start | bytes 12296 | tf_op jit(solution)/shard_map/ppermute | solution.py:521

commit v3 on v2

--- a/solution.py
+++ b/solution.py
@@ -66,27 +66,26 @@
     return total
 
 
-def cut_faces(where, p_ref, faces, *, nz, ny):
-    a_ref, b_ref, c_ref, d_ref = faces
-
+def cut_layers(start, p_ref, out_ref, *, ny):
     def row(y, _):
-        for out_ref, start in ((a_ref, where[A_FROM]), (b_ref, where[B_FROM])):
-            for z in range(H):
-                out_ref[z * ny + y] = p_ref[H + start + z, H + y]
+        for z in range(H):
+            out_ref[z * ny + y] = p_ref[H + start + z, H + y]
         return 0
 
-    lax.fori_loop(0, ny, row, 0, unroll=2)
-    for out_ref, start in ((c_ref, where[C_FROM]), (d_ref, where[D_FROM])):
-        def layer(z, _, out_ref=out_ref, start=start):
-            for j in range(H):
-                out_ref[z * H + j] = p_ref[H + z, H + start + j]
-            return 0
-
-        lax.fori_loop(0, nz, layer, 0, unroll=2)
+    lax.fori_loop(0, ny, row, 0, unroll=4)
+
+
+def cut_rows(start, p_ref, out_ref, *, nz):
+    def layer(z, _):
+        for j in range(H):
+            out_ref[z * H + j] = p_ref[H + z, H + start + j]
+        return 0
+
+    lax.fori_loop(0, nz, layer, 0, unroll=4)
 
 
 def turn_kernel(where, x_ref, k_ref, p_ref, ke_ref, *rest, nz, ny):
-    faces, (k_here, sems, k_sem) = rest[:4], rest[4:]
+    faces, coef, (k_here, sems, k_sem) = rest[:4], rest[4 : 4 + COEFS], rest[4 + COEFS :]
     a_ref, b_ref, c_ref, d_ref = faces
     vectors = p_ref.shape[2]
     k_copy = pltpu.make_async_copy(k_ref, k_here, k_sem)
@@ -102,12 +101,16 @@
     k_turned = permuted(k_here[...].reshape(nz * ny, nx) * (1.0 / half_width), matrix)
     for z in range(nz):
         ke_ref[H + z, pl.ds(PAD + H, ny), :] = k_turned[z * ny : (z + 1) * ny]
+    coefficients(ke_ref, coef, H, nz)
     for copy in copies:
         copy.wait()
     for z in range(0, nz, CHUNK):
         block = p_ref.at[pl.ds(H + z, CHUNK), pl.ds(H, ny)]
         block[...] = permuted(block[...].reshape(CHUNK * ny * vectors, nx), matrix).reshape(CHUNK, ny, vectors, nx)
-    cut_faces(where, p_ref, faces, nz=nz, ny=ny)
+    cut_layers(where[A_FROM], p_ref, a_ref, ny=ny)
+    cut_layers(where[B_FROM], p_ref, b_ref, ny=ny)
+    cut_rows(where[C_FROM], p_ref, c_ref, nz=nz)
+    cut_rows(where[D_FROM], p_ref, d_ref, nz=nz)
     c_low = where[C_FROM] == 0
     for z in range(nz):
         low, high = ke_ref[H + z, pl.ds(PAD + H, H), :], ke_ref[H + z, pl.ds(PAD + ny, H), :]
@@ -298,7 +301,8 @@
 def inner_kernel(where, p_in, *rest, nz, ny, first):
     size = dict(nz=nz, ny=ny)
     if first:
-        ke_in, face_ref, p_ref, ke_ref, q_ref, *coef = rest
+        ke_in, *rest = rest
+        face_ref, p_ref, ke_ref, q_ref, *coef = rest[COEFS:]
         store = None
     else:
         *coef, face_ref, p_ref, q_ref, even_ref, odd_ref = rest
@@ -306,7 +310,7 @@
         store = filtered_store((even_ref, odd_ref), **size)
     fill_face(where, 0, p_ref, ke_ref, face_ref, **size)
     if first:
-        coefficients(ke_ref, coef, near_layers(where), nz + H)
+        coefficients(ke_ref, coef, jnp.where(where[Z_ODD] == 1, 0, H + nz - 1), H + 1)
     steps(where, "inner", coef, p_ref, q_ref, store, **size)
 
 
@@ -314,7 +318,8 @@
     size = dict(nz=nz, ny=ny)
     if first:
         ke_in, *rest = rest
-        corner_ref, p_ref, q_ref, ke_ref, *coef = rest[COEFS:]
+        corner_ref, p_ref, q_ref, ke_ref, *rest = rest[COEFS:]
+        coef, out_ref = rest[:COEFS], rest[COEFS]
         store = None
     else:
         *coef, corner_ref, even_in, odd_in, p_ref, q_ref, even_ref, odd_ref, g_ref = rest
@@ -324,7 +329,9 @@
     if first:
         coefficients(ke_ref, coef, near_layers(where), nz + H, groups=(0, (ny + 2 * H) // 8 - 1))
     steps(where, "edges", coef, p_ref, q_ref, store, **size)
-    if not first:
+    if first:
+        cut_layers(where[A_FROM], p_ref, out_ref, ny=ny)
+    else:
         pairs = products((even_ref, odd_ref), where[A_FROM] * ny // 8, H * ny // 8, nz * ny, None)
         for n, total in enumerate(pairs):
             g_ref[n] = total
@@ -347,7 +354,10 @@
         coefficients(ke_ref, coef, jnp.where(where[Z_ODD] == 1, H + nz - 1, 0), H + 1)
     steps(where, "far", coef, p_ref, q_ref, store, **size)
     if first:
-        cut_faces(where, p_ref, faces, **size)
+        b_ref, c_ref, d_ref = faces
+        cut_layers(where[B_FROM], p_ref, b_ref, ny=ny)
+        cut_rows(where[C_FROM], p_ref, c_ref, nz=nz)
+        cut_rows(where[D_FROM], p_ref, d_ref, nz=nz)
     else:
         sums = products((even_ref, odd_ref), where[B_FROM] * ny // 8, H * ny // 8, nz * ny, pairs_ref)
         row_of = lax.broadcasted_iota(jnp.int32, g_ref.shape, 0)
@@ -463,12 +473,11 @@
     kernel = lambda f, **more: functools.partial(f, nz=nz, ny=ny, **more)
     swap = lambda payload, pairs: lax.ppermute(payload, *pairs)
 
-    def begin(a, b, c, d):
+    def begin(b, c, d):
         c = swap(c, c_pairs)
         d = swap(d, d_pairs)
-        a = swap(a, a_pairs)
         b = swap(b, b_pairs)
-        return a, b, c, d
+        return b, c, d
 
     def corners(p, ke, c, d):
         first = ke is not None
@@ -483,24 +492,26 @@
 
     inner_flops, edge_flops, far_flops = 16_000_000, 4_000_000, 12_000_000
     extra_z, extra_y = H * ny // 8, nz * H // 8
-    p, k, a, b, c, d = call(
+    p, k, a, b, c, d, *coef = call(
         kernel(turn_kernel),
-        [field, ke, (H * ny + extra_z, *row), (H * ny + extra_z, *row), (nz * H + extra_y, *row), (nz * H + extra_y, *row)],
+        [field, ke, (H * ny + extra_z, *row), (H * ny + extra_z, *row), (nz * H + extra_y, *row), (nz * H + extra_y, *row), *weights],
         (where, *(pltpu.with_memory_space_constraint(arg, pltpu.HBM) for arg in (block, conduct))), space=pltpu.HBM,
         scratch=[pltpu.VMEM(conduct.shape, F32), pltpu.SemaphoreType.DMA((vectors,)), pltpu.SemaphoreType.DMA])
-    a, b, c, d = begin(a, b, c, d)
-    p, k, q, *coef = call(kernel(inner_kernel, first=True), [field, ke, field, *weights], (where, p, k, a),
-                          {1: 0, 2: 1}, flops=inner_flops)
+    b, c, d = begin(b, c, d)
+    a = swap(a, a_pairs)
+    p, k, q, *coef = call(kernel(inner_kernel, first=True), [field, ke, field, *weights], (where, p, k, *coef, a),
+                          {1: 0, 2: 1, **{3 + n: 3 + n for n in range(COEFS)}}, flops=inner_flops)
     (p, k), ac, bc = corners(p, k, c, d)
-    p, q, k, *coef = call(
-        kernel(edges_kernel, first=True), [field, field, ke, *weights], (where, p, q, k, *coef, ac),
+    p, q, k, *coef, a = call(
+        kernel(edges_kernel, first=True), [field, field, ke, *weights, (H * ny, *row)], (where, p, q, k, *coef, ac),
         {n + 1: n for n in range(3 + COEFS)}, flops=edge_flops)
+    a = swap(a, a_pairs)
     p, q, k, *rest = call(
         kernel(far_kernel, first=True),
-        [field, field, ke, *weights, (H * ny, *row), (H * ny, *row), (nz * H, *row), (nz * H, *row)],
+        [field, field, ke, *weights, (H * ny, *row), (nz * H, *row), (nz * H, *row)],
         (where, p, q, k, *coef, b, bc), {n + 1: n for n in range(3 + COEFS)}, flops=far_flops)
-    coef, (a, b, c, d) = rest[:COEFS], rest[COEFS:]
-    a, b, c, d = begin(a, b, c, d)
+    coef, (b, c, d) = rest[:COEFS], rest[COEFS:]
+    b, c, d = begin(b, c, d)
     p, q, left, right = call(kernel(inner_kernel, first=False), [field, field, *halves_shape], (where, p, *coef, a),
                              {1: 0}, flops=inner_flops)
     (p,), ac, bc = corners(p, None, c, d)
@@ -526,9 +537,9 @@
         return ((y * line + z) * 2 + core) * ycount + x
 
     planar = [[flat(y, x, z, core) for y in range(planes) for x in range(ycount)] for z in range(line) for core in range(2)]
-    part = jnp.sum(gathered(part, ("gz", "gy"), planar), axis=0)
     lines = [[(y * line + z) * 2 + core for z in range(line)] for y in range(planes) for core in range(2)]
-    return gathered(part, "gz", lines)
+    part = jnp.sum(gathered(part, "gz", lines), axis=0)
+    return gathered(part, ("gz", "gy"), planar)
 
 
 def gathered(part, axes, groups):

time: 94.2 us -> 93.4 us (level)
  transfers between devices with their start and end apart: 13 -> 13, of which waited for: 2 -> 3; matrix products, arithmetic and copies ran while one was open for 0% -> 0% of each run, Pallas kernels for 20% -> 25%
where the time goes in v3:
time: 93.4 us; the launch traced here: 92.5 us
  Pallas kernels  36.4 us (39%)
  blocking collectives  29.8 us (32%)
  starting transfers between devices  23.7 us (25%)
  waiting for transfers between devices  2.13 us (2%)
    pallas_call x9, Pallas kernels, call(): pl.pallas_call(kernel, out_shape=[jax.ShapeDtypeStruct(s, F32) for s in o...  32.3 us
    all_to_all x2, blocking collectives, gathered(): lax.all_to_all(copies, axes, 0, 0, axis_index_groups=groups, tiled=True)  29.8 us
    ppermute x12, starting transfers between devices, shards(): swap = lambda payload, pairs: lax.ppermute(payload, *pairs)  23.6 us
    pallas_call x1, Pallas kernels, basis(): pl.pallas_call(functools.partial(basis_kernel, scale=scale, blocks=blocks...  4.09 us
  transfers between devices with their start and end apart: 13, of which 3 were waited for; matrix products, arithmetic and copies ran while one was open for 0% of the time, Pallas kernels for 25%

profile of v3, /device:TPU:1, one launch (start us, length us, event | category | flops | bytes accessed | tf_op | source)
XLA Modules:
  0.0 92.5 jit_solution(8107992883445413880)
XLA Ops:
  0.0 0.1 stack.39.where
  0.1 4.0 %shard_map.28 = (f32[16,40,8,256]{3,2,1,0:T(8,128)S(1)}, f32[16,56,256]{2,1,0:T(8,128)S(1)}, f32[144,8,256]{2,1,0:T(8,128)S(1)}, f32[144,8,256]{2,1,0:T(8,128)S(...) custom-call(s32[9]{0:T(128)S(1)} %stack.39.where, ...), custom_call_target="tpu_custom_call" | custom-call | bytes 65536 | tf_op jit(solution)/shard_map/pallas_call | solution.py:32
  4.1 3.3 %collective-permute-start = (f32[144,8,256]{2,1,0:T(8,128)S(1)}, f32[144,8,256]{2,1,0:T(8,128)S(1)}, u32[]{:S(2)}, u32[]{:S(2)}) collective-permute-start(f32[144,8,256]{2,1,0:T(8,128)S(1)} %get-tuple-element.63), channel_id=1, source_target_pairs={{0,4},{4,0},{8,12},{12,8},{16,20},{20,16},{24,28},{28,24},{32,36},... | collective-permute-start | bytes 3538952 | tf_op jit(solution)/shard_map/ppermute | solution.py:474
  7.4 1.9 %collective-permute-start.4 = (f32[144,8,256]{2,1,0:T(8,128)S(1)}, f32[144,8,256]{2,1,0:T(8,128)S(1)}, u32[]{:S(2)}, u32[]{:S(2)}) collective-permute-start(f32[144,8,256]{2,1,0:T(8,128)S(1)} %get-tuple-element.83), channel_id=1, source_target_pairs={{4,8},{8,4},{12,16},{16,12},{20,24},{24,20},{28,32},{32,28},{36,40... | collective-permute-start | bytes 3538952 | tf_op jit(solution)/shard_map/ppermute | solution.py:474
  9.3 1.1 %collective-permute-start.1 = (f32[36,8,256]{2,1,0:T(8,128)S(1)}, f32[36,8,256]{2,1,0:T(8,128)S(1)}, u32[]{:S(2)}, u32[]{:S(2)}) collective-permute-start(f32[36,8,256]{2,1,0:T(8,128)S(1)} %get-tuple-element.66), channel_id=1, source_target_pairs={{0,1},{1,0},{2,3},{3,2},{4,5},{5,4},{6,7},{7,6},{8,9},{9,8},{10,11... | collective-permute-start | bytes 884744 | tf_op jit(solution)/shard_map/ppermute | solution.py:474
  10.4 0.7 collective-permute-start.2
  11.1 0.0 collective-permute-done.rest_5_
  11.1 5.7 %shard_map.29 = (f32[16,40,8,256]{3,2,1,0:T(8,128)S(1)}, f32[16,56,256]{2,1,0:T(8,128)S(1)}, f32[16,40,8,256]{3,2,1,0:T(8,128)S(1)}, f32[16,40,256]{2,1,0:T(8,12...) custom-call(s32[9]{0:T(128)S(1)} %stack.39.where, ...), custom_call_target="tpu_custom_call", output_to_operand_aliasing={{0}: (1, {}), {1}: (2, {}), {3}: (3, {}), {4}: (4, {}), {5}... | custom-call | flops 16000000 | bytes 65536 | tf_op jit(solution)/shard_map/pallas_call | solution.py:32
  16.8 0.6 collective-permute-done.1.rest_1_
  17.4 0.0 collective-permute-done.2.rest_2_
  17.4 0.6 shard_map.30
  18.1 0.1 collective-permute-start.3
  18.2 4.6 %collective-permute-start.5 = (f32[14,8,256]{2,1,0:T(8,128)S(1)}, f32[14,8,256]{2,1,0:T(8,128)S(1)}, u32[]{:S(2)}, u32[]{:S(2)}) collective-permute-start(f32[14,8,256]{2,1,0:T(8,128)S(1)} %get-tuple-element.84), channel_id=1, source_target_pairs={{4,8},{8,4},{12,16},{16,12},{20,24},{24,20},{28,32},{32,28},{36,40... | collective-permute-start | bytes 344072 | tf_op jit(solution)/shard_map/ppermute | solution.py:474
  22.8 0.0 collective-permute-done.3.rest_5_
  22.9 2.8 %shard_map.31 = (f32[16,40,8,256]{3,2,1,0:T(8,128)S(1)}, f32[16,40,8,256]{3,2,1,0:T(8,128)S(1)}, f32[16,56,256]{2,1,0:T(8,128)S(1)}, f32[16,40,256]{2,1,0:T(8,12...) custom-call(s32[9]{0:T(128)S(1)} %stack.39.where, ...), custom_call_target="tpu_custom_call", output_to_operand_aliasing={{0}: (1, {}), {1}: (2, {}), {2}: (3, {}), {3}: (4, {}), {4}... | custom-call | flops 4000000 | bytes 65536 | tf_op jit(solution)/shard_map/pallas_call | solution.py:32
  25.7 0.1 collective-permute-start.6
  25.8 0.0 collective-permute-done.4.rest_5_
  25.8 0.3 collective-permute-done.5.rest_6_
  26.1 4.9 %shard_map.32 = (f32[16,40,8,256]{3,2,1,0:T(8,128)S(1)}, f32[16,40,8,256]{3,2,1,0:T(8,128)S(1)}, f32[16,56,256]{2,1,0:T(8,128)S(1)}, f32[16,40,256]{2,1,0:T(8,12...) custom-call(s32[9]{0:T(128)S(1)} %stack.39.where, ...), custom_call_target="tpu_custom_call", output_to_operand_aliasing={{0}: (1, {}), {1}: (2, {}), {2}: (3, {}), {3}: (4, {}), {4}... | custom-call | flops 12000000 | bytes 65536 | tf_op jit(solution)/shard_map/pallas_call | solution.py:32
  31.0 2.8 %collective-permute-start.10 = (f32[128,8,256]{2,1,0:T(8,128)S(1)}, f32[128,8,256]{2,1,0:T(8,128)S(1)}, u32[]{:S(2)}, u32[]{:S(2)}) collective-permute-start(f32[128,8,256]{2,1,0:T(8,128)S(1)} %get-tuple-element.101), channel_id=1, source_target_pairs={{4,8},{8,4},{12,16},{16,12},{20,24},{24,20},{28,32},{32,28},{36,40... | collective-permute-start | bytes 3145736 | tf_op jit(solution)/shard_map/ppermute | solution.py:474
  33.8 3.9 %collective-permute-start.7 = (f32[32,8,256]{2,1,0:T(8,128)S(1)}, f32[32,8,256]{2,1,0:T(8,128)S(1)}, u32[]{:S(2)}, u32[]{:S(2)}) collective-permute-start(f32[32,8,256]{2,1,0:T(8,128)S(1)} %get-tuple-element.92), channel_id=1, source_target_pairs={{0,1},{1,0},{2,3},{3,2},{4,5},{5,4},{6,7},{7,6},{8,9},{9,8},{10,11... | collective-permute-start | bytes 786440 | tf_op jit(solution)/shard_map/ppermute | solution.py:474
  37.7 0.7 collective-permute-start.8
  38.4 0.0 collective-permute-done.6.rest_4_
  38.4 5.7 %shard_map.33 = (f32[16,40,8,256]{3,2,1,0:T(8,128)S(1)}, f32[16,40,8,256]{3,2,1,0:T(8,128)S(1)}, f32[2048,128]{1,0:T(8,128)S(1)}, f32[2048,128]{1,0:T(8,128)S(1)}) custom-call(s32[9]{0:T(128)S(1)} %stack.39.where, f32[16,40,8,256]{3,2,1,0:T(8,128)S(1)} %get-tuple-element.85.p_in, ...), custom_call_target="tpu_custom_call", output_to_operand_aliasing={{0}: (1, {})} | custom-call | flops 16000000 | bytes 65536 | tf_op jit(solution)/shard_map/pallas_call | solution.py:32
  44.1 0.0 collective-permute-done.7.rest_0_
  44.1 0.0 collective-permute-done.8.rest_1_
  44.1 0.6 shard_map.34
  44.7 0.1 collective-permute-start.9
  44.8 4.4 %collective-permute-start.11 = (f32[12,8,256]{2,1,0:T(8,128)S(1)}, f32[12,8,256]{2,1,0:T(8,128)S(1)}, u32[]{:S(2)}, u32[]{:S(2)}) collective-permute-start(f32[12,8,256]{2,1,0:T(8,128)S(1)} %get-tuple-element.102), channel_id=1, source_target_pairs={{4,8},{8,4},{12,16},{16,12},{20,24},{24,20},{28,32},{32,28},{36,40... | collective-permute-start | bytes 294920 | tf_op jit(solution)/shard_map/ppermute | solution.py:474
  49.2 0.0 collective-permute-done.9.rest_4_
  49.2 2.4 %shard_map.35 = (f32[16,40,8,256]{3,2,1,0:T(8,128)S(1)}, f32[16,40,8,256]{3,2,1,0:T(8,128)S(1)}, f32[2048,128]{1,0:T(8,128)S(1)}, f32[2048,128]{1,0:T(8,128)S(1)}, f32[36,8,128]{2,1,0:T(8,128)S(1)}) custom-call(s32[9]{0:T(128)S(1)} %stack.39.where, ...), custom_call_target="tpu_custom_call", output_to_operand_aliasing={{0}: (1, {}), {1}: (2, {}), {2}: (8, {}), {3}: (9, {})} | custom-call | flops 4000000 | bytes 65536 | tf_op jit(solution)/shard_map/pallas_call | solution.py:32
  51.6 0.0 collective-permute-done.10.rest_4_
  51.6 0.0 collective-permute-done.11.rest_5_
  51.6 5.5 %shard_map.36 = (f32[16,40,8,256]{3,2,1,0:T(8,128)S(1)}, f32[16,40,8,256]{3,2,1,0:T(8,128)S(1)}, f32[2048,128]{1,0:T(8,128)S(1)}, f32[2048,128]{1,0:T(8,128)S(1)}, f32[8,128]{1,0:T(8,128)S(1)}) custom-call(s32[9]{0:T(128)S(1)} %stack.39.where, ...), custom_call_target="tpu_custom_call", output_to_operand_aliasing={{0}: (1, {}), {1}: (2, {}), {2}: (9, {}), {3}: (10, {})} | custom-call | flops 12000000 | bytes 65536 | tf_op jit(solution)/shard_map/pallas_call | solution.py:32
  57.2 0.1 collective-permute-start.12
  57.3 1.2 %collective-permute-done.12 = f32[8,128]{1,0:T(8,128)S(1)} collective-permute-done((f32[8,128]{1,0:T(8,128)S(1)}, f32[8,128]{1,0:T(8,128)S(1)}, u32[]{:S(2)}, u32[]{:S(2)}) %collective-permute-start.12) | collective-permute-done | bytes 4128 | tf_op jit(solution)/shard_map/ppermute | solution.py:532
  58.4 16.0 %all_to_all.10 = f32[8,8,128]{2,1,0:T(8,128)S(1)} all-to-all(f32[8,8,128]{2,1,0:T(8,128)S(1)} %broadcast_in_dim.4), channel_id=1, replica_groups={{0,8,16,24,32,40,48,56},{4,12,20,28,36,44,52,60},{64,72,80,88,96,104,11..., dimensions={0} | all-to-all | bytes 65536 | tf_op jit(solution)/shard_map/all_to_all | solution.py:548
  74.4 13.8 %all_to_all.11.g_ref = f32[16,8,128]{2,1,0:T(8,128)S(1)} all-to-all(f32[16,8,128]{2,1,0:T(8,128)S(1)} %broadcast_in_dim.5), channel_id=1, replica_groups={{0,1,2,3,64,65,66,67,128,129,130,131,192,193,194,195},{4,5,6,7,68,69,70..., dimensions={0} | all-to-all | bytes 131072 | tf_op jit(solution)/shard_map/all_to_all | solution.py:548
  88.2 4.1 %basis.1 = f32[8,256,256]{2,1,0:T(8,128)} custom-call(f32[16,8,128]{2,1,0:T(8,128)S(1)} %all_to_all.11.g_ref, f32[8,256,128]{2,1,0:T(8,128)S(1)} %bitcast.12, f32[8,256,128]{2,1,0:T(8,128)S(1)} %bitcast.13), custom_call_target="tpu_custom_call" | custom-call | tf_op jit(solution)/shard_map/basis/pallas_call | solution.py:443
  (4 shorter events, 0.0 us)
Async XLA Ops:
  4.1 7.0 %collective-permute-start = (f32[144,8,256]{2,1,0:T(8,128)S(1)}, f32[144,8,256]{2,1,0:T(8,128)S(1)}, u32[]{:S(2)}, u32[]{:S(2)}) collective-permute-start(f32[144,8,256]{2,1,0:T(8,128)S(1)} %get-tuple-element.63), channel_id=1, source_target_pairs={{0,4},{4,0},{8,12},{12,8},{16,20},{20,16},{24,28},{28,24},{32,36},... | collective-permute-start | bytes 3538952 | tf_op jit(solution)/shard_map/ppermute | solution.py:474
  7.4 18.4 %collective-permute-start.4 = (f32[144,8,256]{2,1,0:T(8,128)S(1)}, f32[144,8,256]{2,1,0:T(8,128)S(1)}, u32[]{:S(2)}, u32[]{:S(2)}) collective-permute-start(f32[144,8,256]{2,1,0:T(8,128)S(1)} %get-tuple-element.83), channel_id=1, source_target_pairs={{4,8},{8,4},{12,16},{16,12},{20,24},{24,20},{28,32},{32,28},{36,40... | collective-permute-start | bytes 3538952 | tf_op jit(solution)/shard_map/ppermute | solution.py:474
  9.3 8.1 %collective-permute-start.1 = (f32[36,8,256]{2,1,0:T(8,128)S(1)}, f32[36,8,256]{2,1,0:T(8,128)S(1)}, u32[]{:S(2)}, u32[]{:S(2)}) collective-permute-start(f32[36,8,256]{2,1,0:T(8,128)S(1)} %get-tuple-element.66), channel_id=1, source_target_pairs={{0,1},{1,0},{2,3},{3,2},{4,5},{5,4},{6,7},{7,6},{8,9},{9,8},{10,11... | collective-permute-start | bytes 884744 | tf_op jit(solution)/shard_map/ppermute | solution.py:474
  10.4 7.0 %collective-permute-start.2 = (f32[36,8,256]{2,1,0:T(8,128)S(1)}, f32[36,8,256]{2,1,0:T(8,128)S(1)}, u32[]{:S(2)}, u32[]{:S(2)}) collective-permute-start(f32[36,8,256]{2,1,0:T(8,128)S(1)} %get-tuple-element.67), channel_id=1, source_target_pairs={{1,2},{2,1},{5,6},{6,5},{9,10},{10,9},{13,14},{14,13},{17,18},{18,... | collective-permute-start | bytes 884744 | tf_op jit(solution)/shard_map/ppermute | solution.py:474
  18.1 4.8 %collective-permute-start.3 = (f32[14,8,256]{2,1,0:T(8,128)S(1)}, f32[14,8,256]{2,1,0:T(8,128)S(1)}, u32[]{:S(2)}, u32[]{:S(2)}) collective-permute-start(f32[14,8,256]{2,1,0:T(8,128)S(1)} %get-tuple-element.75), channel_id=1, source_target_pairs={{0,4},{4,0},{8,12},{12,8},{16,20},{20,16},{24,28},{28,24},{32,36},... | collective-permute-start | bytes 344072 | tf_op jit(solution)/shard_map/ppermute | solution.py:474
  18.2 8.0 %collective-permute-start.5 = (f32[14,8,256]{2,1,0:T(8,128)S(1)}, f32[14,8,256]{2,1,0:T(8,128)S(1)}, u32[]{:S(2)}, u32[]{:S(2)}) collective-permute-start(f32[14,8,256]{2,1,0:T(8,128)S(1)} %get-tuple-element.84), channel_id=1, source_target_pairs={{4,8},{8,4},{12,16},{16,12},{20,24},{24,20},{28,32},{32,28},{36,40... | collective-permute-start | bytes 344072 | tf_op jit(solution)/shard_map/ppermute | solution.py:474
  25.7 12.7 %collective-permute-start.6 = (f32[128,8,256]{2,1,0:T(8,128)S(1)}, f32[128,8,256]{2,1,0:T(8,128)S(1)}, u32[]{:S(2)}, u32[]{:S(2)}) collective-permute-start(f32[128,8,256]{2,1,0:T(8,128)S(1)} %get-tuple-element.90), channel_id=1, source_target_pairs={{0,4},{4,0},{8,12},{12,8},{16,20},{20,16},{24,28},{28,24},{32,36},... | collective-permute-start | bytes 3145736 | tf_op jit(solution)/shard_map/ppermute | solution.py:474
  31.0 20.6 %collective-permute-start.10 = (f32[128,8,256]{2,1,0:T(8,128)S(1)}, f32[128,8,256]{2,1,0:T(8,128)S(1)}, u32[]{:S(2)}, u32[]{:S(2)}) collective-permute-start(f32[128,8,256]{2,1,0:T(8,128)S(1)} %get-tuple-element.101), channel_id=1, source_target_pairs={{4,8},{8,4},{12,16},{16,12},{20,24},{24,20},{28,32},{32,28},{36,40... | collective-permute-start | bytes 3145736 | tf_op jit(solution)/shard_map/ppermute | solution.py:474
  33.8 10.2 %collective-permute-start.7 = (f32[32,8,256]{2,1,0:T(8,128)S(1)}, f32[32,8,256]{2,1,0:T(8,128)S(1)}, u32[]{:S(2)}, u32[]{:S(2)}) collective-permute-start(f32[32,8,256]{2,1,0:T(8,128)S(1)} %get-tuple-element.92), channel_id=1, source_target_pairs={{0,1},{1,0},{2,3},{3,2},{4,5},{5,4},{6,7},{7,6},{8,9},{9,8},{10,11... | collective-permute-start | bytes 786440 | tf_op jit(solution)/shard_map/ppermute | solution.py:474
  37.7 6.4 %collective-permute-start.8 = (f32[32,8,256]{2,1,0:T(8,128)S(1)}, f32[32,8,256]{2,1,0:T(8,128)S(1)}, u32[]{:S(2)}, u32[]{:S(2)}) collective-permute-start(f32[32,8,256]{2,1,0:T(8,128)S(1)} %get-tuple-element.93), channel_id=1, source_target_pairs={{1,2},{2,1},{5,6},{6,5},{9,10},{10,9},{13,14},{14,13},{17,18},{18,... | collective-permute-start | bytes 786440 | tf_op jit(solution)/shard_map/ppermute | solution.py:474
  44.7 4.5 %collective-permute-start.9 = (f32[12,8,256]{2,1,0:T(8,128)S(1)}, f32[12,8,256]{2,1,0:T(8,128)S(1)}, u32[]{:S(2)}, u32[]{:S(2)}) collective-permute-start(f32[12,8,256]{2,1,0:T(8,128)S(1)} %get-tuple-element.96), channel_id=1, source_target_pairs={{0,4},{4,0},{8,12},{12,8},{16,20},{20,16},{24,28},{28,24},{32,36},... | collective-permute-start | bytes 294920 | tf_op jit(solution)/shard_map/ppermute | solution.py:474
  44.8 6.8 %collective-permute-start.11 = (f32[12,8,256]{2,1,0:T(8,128)S(1)}, f32[12,8,256]{2,1,0:T(8,128)S(1)}, u32[]{:S(2)}, u32[]{:S(2)}) collective-permute-start(f32[12,8,256]{2,1,0:T(8,128)S(1)} %get-tuple-element.102), channel_id=1, source_target_pairs={{4,8},{8,4},{12,16},{16,12},{20,24},{24,20},{28,32},{32,28},{36,40... | collective-permute-start | bytes 294920 | tf_op jit(solution)/shard_map/ppermute | solution.py:474
  57.2 1.3 %collective-permute-start.12 = (f32[8,128]{1,0:T(8,128)S(1)}, f32[8,128]{1,0:T(8,128)S(1)}, u32[]{:S(2)}, u32[]{:S(2)}) collective-permute-start(f32[8,128]{1,0:T(8,128)S(1)} %get-tuple-element.106), channel_id=1, source_target_pairs={{0,4},{4,0},{8,12},{12,8},{16,20},{20,16},{24,28},{28,24},{32,36},... | collective-permute-start | bytes 12296 | tf_op jit(solution)/shard_map/ppermute | solution.py:532
